TPU v7x, 512 devices: a whole 4x8x8 slice. The times are simulated.
512 devices in a mesh: dp: 32 (over x, z), hidden: 16 (over y, core).
Axes of the slice: x: 4, y: 8, z: 8, core: 2. Of those that a mesh axis runs over, the one named last changes fastest.
Arguments:
- activations: bfloat16 [4096, 768], P(('dp', 'hidden')), may hold values from -6 to 6
- grad_out: bfloat16 [4096, 53248], P('dp', 'hidden'), may hold values from -8 to 8
- momentum: float32 [768, 53248], P('dp', 'hidden'), may hold values from -6 to 6
Outputs:
- new_momentum: float32 [768, 53248], P('dp', 'hidden')
All inputs are finite; a program needn't handle non-finite values.
Results may differ from a plain program's by a relative error of at most 0.0003.
Values may be sent and summed in bfloat16 or wider, within the bound.
No kernel may reach another device: no remote copies, remote signals or barrier semaphores. Data moves between devices by JAX's collectives and lax.ppermute only.
A program may use at most 64 MiB of HBM per device.

v0:
```python
import jax
import jax.numpy as jnp
from jax import lax
from jax.sharding import PartitionSpec as P

EPSILON = 1e-06
DECAY = 0.9


def from_partner(shard, axis, bit):
    return lax.ppermute(shard, axis, [(i, i ^ 1 << bit) for i in range(lax.axis_size(axis))])


def group_sums(partial_value, replica, level_index, n_replicas):
    n_groups = n_replicas >> level_index + 1
    group_id = replica >> level_index + 1
    selector = (jnp.arange(n_groups, dtype=jnp.int32) == group_id).astype(jnp.float32)
    slot_table = selector[:, None] * partial_value[None, :]
    summed = lax.psum(slot_table, ("dp", "hidden"))
    result = jnp.sum(summed * selector[:, None], axis=0)
    return result


def blend(kept_half, came_half, own_bit, replica, level_index, n_replicas):
    kept_sq = jnp.sum(kept_half * kept_half)
    came_sq = jnp.sum(came_half * came_half)
    cross = jnp.sum(kept_half * came_half)
    lower_first = own_bit == 0
    partial_value = jnp.stack(
        [jnp.where(lower_first, kept_sq, came_sq), jnp.where(lower_first, came_sq, kept_sq), cross]
    )
    sums = group_sums(partial_value, replica, level_index, n_replicas)
    lower_coef = 1.0 - sums[2] / (2.0 * (sums[0] + EPSILON))
    upper_coef = 1.0 - sums[2] / (2.0 * (sums[1] + EPSILON))
    kept_coef = jnp.where(lower_first, lower_coef, upper_coef)
    came_coef = jnp.where(lower_first, upper_coef, lower_coef)
    return kept_coef * kept_half + came_coef * came_half


def split_pair(blocks, own_bit):
    paired = blocks.reshape(blocks.shape[0] // 2, 2, blocks.shape[1], blocks.shape[2])
    kept_half = lax.dynamic_index_in_dim(paired, own_bit, 1, keepdims=False)
    given_half = lax.dynamic_index_in_dim(paired, 1 - own_bit, 1, keepdims=False)
    return (kept_half, given_half)


def contract(left_rows, upstream):
    return lax.dot_general(
        left_rows, upstream, (((0,), (0,)), ((), ())), preferred_element_type=jnp.float32
    )


def local(activations, grad_out, momentum):
    n_replicas = lax.axis_size("dp")
    levels = n_replicas.bit_length() - 1
    replica = lax.axis_index("dp")
    rows_window = activations.shape[1]
    block_rows = rows_window // n_replicas
    columns = grad_out.shape[1]
    gradient = contract(lax.all_gather(activations, "hidden", axis=0, tiled=True), grad_out)
    current = gradient.reshape(n_replicas, block_rows, columns)
    start_level = 0
    for level_index in range(start_level, levels):
        own_bit = (replica >> level_index) % 2
        kept_half, given_half = split_pair(current, own_bit)
        came_half = from_partner(given_half, "dp", level_index)
        current = blend(kept_half, came_half, own_bit, replica, level_index, n_replicas)
    return DECAY * momentum + current.reshape(block_rows, columns)


def solution(mesh):
    return jax.shard_map(
        local,
        mesh=mesh,
        in_specs=(P(("dp", "hidden"), None), P("dp", "hidden"), P("dp", "hidden")),
        out_specs=P("dp", "hidden"),
        check_vma=False,
    )
```

profile of v0, /device:TPU:1, one launch (start us, length us, event | category | flops | bytes accessed | tf_op | source)
XLA Modules:
  0.0 894.3 jit_solution(13523488133192906090)
XLA Ops:
  0.0 21.8 %all_gather.3 = bf16[128,768]{1,0:T(8,128)(2,1)S(1)} all-gather(bf16[8,768]{1,0:T(8,128)(2,1)} %param.3), channel_id=1, replica_groups=mesh['dp'=32,'hidden'=16] {'hidden'}, dimensions={0}, use_global_device_ids=true | all-gather | bytes 208896 | tf_op jit(solution)/shard_map/all_gather | solution.py:60
  23.3 2.8 dynamic-slice_bitcast_fusion
  26.1 2.6 copy-done.1
  28.7 2.0 collective-permute-start
  30.8 111.8 %collective-permute-done = f32[16,24,3328]{2,1,0:T(8,128)} collective-permute-done((f32[16,24,3328]{2,1,0:T(8,128)}, f32[16,24,3328]{2,1,0:T(8,128)}, u32[]{:S(2)}, u32[]{:S(2)}) %collective-permute-start) | collective-permute-done | bytes 5111840 | tf_op jit(solution)/shard_map/ppermute | solution.py:11
  142.5 5.9 fusion
  151.7 100.7 %psum.35 = f32[16,3]{0,1:T(4,128)S(1)} all-reduce(f32[16,3]{0,1:T(4,128)S(1)} %broadcast_multiply_fusion.2), channel_id=1, replica_groups=mesh['dp'=32,'hidden'=16] {'dp','hidden'}, use_global_device_ids=true, to_apply=%region_3.4 | all-reduce | flops 48 | bytes 384 | tf_op jit(solution)/shard_map/psum | solution.py:19
  255.7 4.6 fusion.2
  263.3 1.9 collective-permute-start.1
  265.3 112.6 %collective-permute-done.1 = f32[8,24,3328]{2,1,0:T(8,128)S(1)} collective-permute-done((f32[8,24,3328]{2,1,0:T(8,128)}, f32[8,24,3328]{2,1,0:T(8,128)S(1)}, u32[]{:S(2)}, u32[]{:S(2)}) %collective-permute-start.1) | collective-permute-done | bytes 2555936 | tf_op jit(solution)/shard_map/ppermute | solution.py:11
  377.9 4.0 fusion.3
  385.2 94.0 %psum.36 = f32[8,3]{0,1:T(4,128)S(1)} all-reduce(f32[8,3]{0,1:T(4,128)S(1)} %broadcast_multiply_fusion.1), channel_id=1, replica_groups=mesh['dp'=32,'hidden'=16] {'dp','hidden'}, use_global_device_ids=true, to_apply=%region_8.9 | all-reduce | flops 24 | bytes 192 | tf_op jit(solution)/shard_map/psum | solution.py:19
  482.5 2.8 fusion.5
  486.4 3.9 collective-permute-start.2
  490.3 58.8 %collective-permute-done.2 = f32[4,24,3328]{2,1,0:T(8,128)} collective-permute-done((f32[4,24,3328]{2,1,0:T(8,128)}, f32[4,24,3328]{2,1,0:T(8,128)}, u32[]{:S(2)}, u32[]{:S(2)}) %collective-permute-start.2) | collective-permute-done | bytes 1277984 | tf_op jit(solution)/shard_map/ppermute | solution.py:11
  549.1 2.3 fusion.6
  554.9 96.0 %psum.37 = f32[4,3]{1,0:T(4,128)S(1)} all-reduce(f32[4,3]{1,0:T(4,128)S(1)} %broadcast_multiply_fusion), channel_id=1, replica_groups=mesh['dp'=32,'hidden'=16] {'dp','hidden'}, use_global_device_ids=true, to_apply=%region_13.14 | all-reduce | flops 12 | bytes 96 | tf_op jit(solution)/shard_map/psum | solution.py:19
  656.8 2.9 collective-permute-start.3
  659.8 14.3 %collective-permute-done.3 = f32[2,24,3328]{2,1,0:T(8,128)S(1)} collective-permute-done((f32[2,24,3328]{2,1,0:T(8,128)S(1)}, f32[2,24,3328]{2,1,0:T(8,128)S(1)}, u32[]{:S(2)}, u32[]{:S(2)}) %collective-permute-start.3) | collective-permute-done | bytes 639008 | tf_op jit(solution)/shard_map/ppermute | solution.py:11
  674.1 1.9 fusion.9
  679.4 95.3 %psum.38 = f32[2,3]{1,0:T(2,128)S(1)} all-reduce(f32[2,3]{1,0:T(2,128)S(1)} %broadcast_multiply_fusion.3), channel_id=1, replica_groups=mesh['dp'=32,'hidden'=16] {'dp','hidden'}, use_global_device_ids=true, to_apply=%region_18.19 | all-reduce | flops 6 | bytes 48 | tf_op jit(solution)/shard_map/psum | solution.py:19
  779.3 2.9 collective-permute-start.4
  782.2 8.9 collective-permute-done.4
  795.1 95.3 %psum.39 = f32[1,3]{1,0:T(1,128)S(1)} all-reduce(f32[1,3]{1,0:T(1,128)S(1)} %maximum_multiply_fusion), channel_id=1, replica_groups=mesh['dp'=32,'hidden'=16] {'dp','hidden'}, use_global_device_ids=true, to_apply=%region_23.24 | all-reduce | flops 3 | bytes 24 | tf_op jit(solution)/shard_map/psum | solution.py:19
  (43 shorter events, 18.3 us)
Async XLA Ops:
  0.0 21.8 %copy-start = (bf16[128,3328]{1,0:T(8,128)(2,1)S(1)}, bf16[128,3328]{1,0:T(8,128)(2,1)}, u32[]{:S(2)}) copy-start(bf16[128,3328]{1,0:T(8,128)(2,1)} %param.4) | copy-start | bytes 2555908
  23.3 5.4 copy-start.1
  28.7 113.8 %collective-permute-start = (f32[16,24,3328]{2,1,0:T(8,128)}, f32[16,24,3328]{2,1,0:T(8,128)}, u32[]{:S(2)}, u32[]{:S(2)}) collective-permute-start(f32[16,24,3328]{2,1,0:T(8,128)} %dynamic-slice_bitcast_fusion), channel_id=1, source_target_pairs={{0,16},{16,0},{32,48},{48,32},{64,80},{80,64},{96,112},{112,96},{1... | collective-permute-start | bytes 15335432 | tf_op jit(solution)/shard_map/ppermute | solution.py:11
  260.3 3.0 copy-start.2
  263.3 114.5 %collective-permute-start.1 = (f32[8,24,3328]{2,1,0:T(8,128)}, f32[8,24,3328]{2,1,0:T(8,128)S(1)}, u32[]{:S(2)}, u32[]{:S(2)}) collective-permute-start(f32[8,24,3328]{2,1,0:T(8,128)} %dynamic-slice_bitcast_fusion.1), channel_id=1, source_target_pairs={{0,32},{16,48},{32,0},{48,16},{64,96},{80,112},{96,64},{112,80},{1... | collective-permute-start | bytes 7667720 | tf_op jit(solution)/shard_map/ppermute | solution.py:11
  377.9 4.0 copy-start.3
  486.4 62.7 %collective-permute-start.2 = (f32[4,24,3328]{2,1,0:T(8,128)}, f32[4,24,3328]{2,1,0:T(8,128)}, u32[]{:S(2)}, u32[]{:S(2)}) collective-permute-start(f32[4,24,3328]{2,1,0:T(8,128)} %dynamic-slice_bitcast_fusion.2), channel_id=1, source_target_pairs={{0,64},{16,80},{32,96},{48,112},{64,0},{80,16},{96,32},{112,48},{1... | collective-permute-start | bytes 3833864 | tf_op jit(solution)/shard_map/ppermute | solution.py:11
  655.7 1.0 copy-start.4
  656.8 236.8 %copy-start.5 = (f32[24,3328]{1,0:T(8,128)S(1)}, f32[24,3328]{1,0:T(8,128)}, u32[]{:S(2)}) copy-start(f32[24,3328]{1,0:T(8,128)} %param.5) | copy-start | bytes 958468
  656.8 17.3 %collective-permute-start.3 = (f32[2,24,3328]{2,1,0:T(8,128)S(1)}, f32[2,24,3328]{2,1,0:T(8,128)S(1)}, u32[]{:S(2)}, u32[]{:S(2)}) collective-permute-start(f32[2,24,3328]{2,1,0:T(8,128)S(1)} %dynamic-slice_bitcast_fusion.3), channel_id=1, source_target_pairs={{0,128},{16,144},{32,160},{48,176},{64,192},{80,208},{96,224},{112... | collective-permute-start | bytes 1916936 | tf_op jit(solution)/shard_map/ppermute | solution.py:11
  779.3 11.8 %collective-permute-start.4 = (f32[1,24,3328]{2,1,0:T(8,128)S(1)}, f32[1,24,3328]{2,1,0:T(8,128)S(1)}, u32[]{:S(2)}, u32[]{:S(2)}) collective-permute-start(f32[1,24,3328]{2,1,0:T(8,128)S(1)} %constant_dynamic-slice_fusion), channel_id=1, source_target_pairs={{0,256},{16,272},{32,288},{48,304},{64,320},{80,336},{96,352},{112... | collective-permute-start | bytes 958472 | tf_op jit(solution)/shard_map/ppermute | solution.py:11
where the time goes:
time: 895 us; the launch traced here: 894 us
  blocking collectives  503 us (56%)
  waiting for transfers between devices  306 us (34%)
  other arithmetic  29.8 us (3%)
  between operations  26 us (3%)
  local copies, waits for them, and re-layouts  14 us (2%)
  starting transfers between devices  13.6 us (2%)
    psum x5, blocking collectives, group_sums(): summed = lax.psum(slot_table, ('dp', 'hidden'))  481 us
    ppermute x5, waiting for transfers between devices, from_partner(): lax.ppermute(shard, axis, [(i, i ^ 1 << bit) for i in range(lax.axis_size...  306 us
    all_gather x1, blocking collectives, local(): lax.all_gather(activations, 'hidden', axis=0, tiled=True)  21.8 us
  transfers between devices with their start and end apart: 5, of which 5 were waited for; matrix products, arithmetic and copies ran while one was open for 0% of the time, Pallas kernels for 0%

commit v1 on v0

v1 whole, which is shorter than its diff:
```python
import functools

import jax
import jax.numpy as jnp
from jax import lax
from jax.experimental import pallas as pl
from jax.experimental.pallas import tpu as pltpu
from jax.sharding import Mesh, PartitionSpec as P

EPSILON = 1e-06
DECAY = 0.9
NR = 32
TOK = 128
LANES = 128
XZ = ("x", "z")
CORES = [(0, 1), (1, 0)]


def gram_kernel(own_ref, oth_ref, a_ref, g_out_ref, gram_ref, g_ref, q_ref):
    r = pl.program_id(0)
    cols = own_ref.shape[1]
    depth = a_ref.shape[-1]
    act = a_ref[...].reshape(TOK, depth)
    for part, ref in enumerate((own_ref, oth_ref)):
        block = jnp.dot(ref[0], act, preferred_element_type=jnp.float32)
        g_ref[r, pl.ds(part * cols, cols), :] = block
        g_out_ref[0, pl.ds(part * cols, cols), :] = block

    @pl.when(r == NR - 1)
    def _():
        q_ref[...] = jnp.zeros_like(q_ref)
        groups = 2 * cols // 8
        lane_blocks = depth // LANES

        def pair_block(rb, sb):
            def body(f, acc):
                acc = list(acc)
                for half in range(2):
                    row = pl.multiple_of((f * 2 + half) * 8, 8)
                    for lb in range(lane_blocks):
                        lanes = slice(lb * LANES, (lb + 1) * LANES)
                        left = [g_ref[rb * 4 + i, pl.ds(row, 8), lanes] for i in range(4)]
                        right = [g_ref[sb * 4 + i, pl.ds(row, 8), lanes] for i in range(4)]
                        for i in range(4):
                            for j in range(4):
                                acc[i * 4 + j] = acc[i * 4 + j] + left[i] * right[j]
                return tuple(acc)

            zero = jnp.zeros((8, LANES), jnp.float32)
            acc = lax.fori_loop(0, groups // 2, body, (zero,) * 16)
            for i in range(4):
                left_id = rb * 4 + i
                base = lax.rem(left_id, 8) * 128 + lax.div(left_id, 8) * 32
                for j in range(4):
                    q_ref[pl.ds(base + sb * 4 + j, 1), :] = jnp.sum(
                        acc[i * 4 + j], axis=0, keepdims=True
                    )

        def outer(rb, carry):
            def inner(sb, c):
                pair_block(rb, sb)
                return c

            return lax.fori_loop(rb, NR // 4, inner, carry)

        lax.fori_loop(0, NR // 4, outer, 0)
        sums = lax.dot_general(
            jnp.ones((8, LANES), jnp.float32),
            q_ref[...],
            (((1,), (1,)), ((), ())),
            precision=lax.Precision.HIGHEST,
            preferred_element_type=jnp.float32,
        )
        for i in range(8):
            gram_ref[i : i + 1, :] = sums[i : i + 1, i * LANES : (i + 1) * LANES]


def tree_weights(packed):
    gram = jnp.concatenate([packed[:, 32 * q : 32 * q + 32] for q in range(4)], axis=0)
    rows = lax.broadcasted_iota(jnp.int32, (NR, NR), 0)
    cols = lax.broadcasted_iota(jnp.int32, (NR, NR), 1)
    upper = jnp.where(rows < cols, gram, 0.0)
    quad = jnp.where(rows == cols, gram, 2.0 * upper)
    w_col = jnp.ones((NR, 1), jnp.float32)
    w_row = jnp.ones((1, NR), jnp.float32)
    for level in range(5):
        scale = w_col * w_row
        same_half = (rows >> level) == (cols >> level)
        same_pair = (rows >> (level + 1)) == (cols >> (level + 1))
        squares = jnp.where(same_half, quad * scale, 0.0)
        crosses = jnp.where(same_pair & (~same_half), upper * scale, 0.0)

        def both(values, mask):
            down = jnp.sum(values, axis=1, keepdims=True)
            across = jnp.sum(values, axis=0, keepdims=True)
            as_row = jnp.sum(jnp.where(mask, down, 0.0), axis=0, keepdims=True)
            as_col = jnp.sum(jnp.where(mask, across, 0.0), axis=1, keepdims=True)
            return as_col, as_row

        sq_col, sq_row = both(squares, same_half)
        cr_col, cr_row = both(crosses, same_pair)
        w_col = w_col * (1.0 - cr_col / (2.0 * (sq_col + EPSILON)))
        w_row = w_row * (1.0 - cr_row / (2.0 * (sq_row + EPSILON)))
    return w_col


def combine_kernel(part_ref, g_ref, c_ref, w_ref, ct_ref):
    step = pl.program_id(0)
    block = g_ref.shape[1]
    depth = g_ref.shape[2]
    cols = (pl.num_programs(0) * block) // 2

    @pl.when(step == 0)
    def _():
        packed = part_ref[0]
        for k in range(1, part_ref.shape[0]):
            packed = packed + part_ref[k]
        w_ref[...] = jnp.broadcast_to(tree_weights(packed), (NR, LANES))
        ct_ref[pl.ds(ct_ref.shape[0] - 48, 48), :] = jnp.zeros((48, depth), jnp.float32)

    for lb in range(depth // LANES):
        lanes = slice(lb * LANES, (lb + 1) * LANES)
        acc = g_ref[0, :, lanes] * w_ref[0:1, :]
        for r in range(1, NR):
            acc = acc + g_ref[r, :, lanes] * w_ref[r : r + 1, :]
        ct_ref[pl.ds(pl.multiple_of(step * block, 8), block), lanes] = acc

    @pl.when(step == pl.num_programs(0) - 1)
    def _():
        for part in range(2):
            for lb in range(depth // LANES):
                lanes = slice(lb * LANES, (lb + 1) * LANES)
                piece = ct_ref[104 * part : 104 * part + LANES, lanes]
                c_ref[part, lanes, :] = piece.T


def finish_kernel(pieces_ref, momentum_ref, out_ref):
    width = momentum_ref.shape[1] // pieces_ref.shape[0]
    row = jnp.concatenate([pieces_ref[k][:, :width] for k in range(pieces_ref.shape[0])], axis=1)
    out_ref[...] = DECAY * momentum_ref[...] + row


def local(activations, grad_out, momentum):
    core = lax.axis_index("core")
    columns = grad_out.shape[1]
    share = columns // NR
    depth = activations.shape[1] // 2

    halves = activations.reshape(8, 2, depth).transpose(1, 0, 2)
    halves = jnp.broadcast_to(halves[None], (NR, 2, 8, depth)).reshape(2 * NR, 8, depth)
    halves = lax.all_to_all(halves, ("x", "z", "core"), 0, 0, tiled=True)
    acts = lax.all_gather(halves.reshape(NR * 16, depth), "y", axis=0, tiled=True)
    acts = acts.reshape(8, NR, 16, depth)

    own = lax.all_to_all(grad_out.T.reshape(NR, share, TOK), XZ, 0, 0, tiled=True)
    other = lax.ppermute(own, "core", CORES)

    grads, gram = pl.pallas_call(
        gram_kernel,
        grid=(NR,),
        in_specs=[
            pl.BlockSpec((1, share, TOK), lambda r: (r, 0, 0)),
            pl.BlockSpec((1, share, TOK), lambda r: (r, 0, 0)),
            pl.BlockSpec((8, 1, 16, depth), lambda r: (0, r, 0, 0)),
        ],
        out_specs=[
            pl.BlockSpec((1, 2 * share, depth), lambda r: (r, 0, 0)),
            pl.BlockSpec((8, LANES), lambda r: (0, 0)),
        ],
        out_shape=[
            jax.ShapeDtypeStruct((NR, 2 * share, depth), jnp.float32),
            jax.ShapeDtypeStruct((8, LANES), jnp.float32),
        ],
        scratch_shapes=[
            pltpu.VMEM((NR, 2 * share, depth), jnp.float32),
            pltpu.VMEM((1024, LANES), jnp.float32),
        ],
        name="gram",
    )(own, other, acts)

    gram = lax.all_to_all(jnp.broadcast_to(gram, (16, 8, LANES)), ("z", "core"), 0, 0, tiled=True)
    gram = jnp.sum(gram, axis=0)
    gram = lax.all_to_all(jnp.broadcast_to(gram, (32, 8, LANES)), ("x", "y"), 0, 0, tiled=True)

    block = 16
    combined = pl.pallas_call(
        combine_kernel,
        grid=(2 * share // block,),
        in_specs=[
            pl.BlockSpec((32, 8, LANES), lambda f: (0, 0, 0)),
            pl.BlockSpec((NR, block, depth), lambda f: (0, f, 0)),
        ],
        out_specs=pl.BlockSpec((2, depth, LANES), lambda f: (0, 0, 0)),
        out_shape=jax.ShapeDtypeStruct((2, depth, LANES), jnp.float32),
        scratch_shapes=[
            pltpu.VMEM((NR, LANES), jnp.float32),
            pltpu.VMEM((256, depth), jnp.float32),
        ],
        name="combine",
    )(gram, grads)

    mine = combined[0]
    came = lax.ppermute(combined[1], "core", CORES)
    low = jnp.where(core == 0, mine, came)
    high = jnp.where(core == 0, came, mine)
    pieces = jnp.concatenate([low, high], axis=0).reshape(NR, 24, LANES)
    pieces = lax.all_to_all(pieces, XZ, 0, 0, tiled=True)

    return pl.pallas_call(
        finish_kernel,
        out_shape=jax.ShapeDtypeStruct(momentum.shape, jnp.float32),
        name="finish",
    )(pieces, momentum)


def solution(mesh):
    devices = mesh.devices.reshape(4, 8, 8, 2)
    fine = Mesh(devices, ("x", "z", "y", "core"))
    dp, hidden = ("x", "z"), ("y", "core")
    return jax.shard_map(
        local,
        mesh=fine,
        in_specs=(P(dp + hidden, None), P(dp, hidden), P(dp, hidden)),
        out_specs=P(dp, hidden),
        check_vma=False,
    )
```

time: 895 us -> 198 us (0.22)
  blocking collectives: 503 us -> 104 us
  waiting for transfers between devices: 306 us -> 10.6 us
  Pallas kernels: 0 us -> 51.4 us
  other arithmetic: 29.8 us -> 1 us
  between operations: 26 us -> 13.4 us
  local copies, waits for them, and re-layouts: 14 us -> 3.93 us
    psum x5 -> x0, blocking collectives: 481 us -> none  [group_sums(): summed = lax.psum(slot_table, ('dp', 'hidden'))]
    ppermute x5 -> x2, waiting for transfers between devices: 306 us -> 3.03 us  [the longest x1 1.98 us: local(): other = lax.ppermute(own, 'core', CORES)]
    all_to_all x0 -> x5, blocking collectives: none -> 104 us  [the longest x1 29.3 us: local(): halves = lax.all_to_all(halves, ('x', 'z', 'core'), 0, 0, tiled=True)]
    pallas_call x0 -> x3, Pallas kernels: none -> 51.4 us  [the longest x1 39 us: local(): pl.pallas_call(gram_kernel, grid=(NR,), in_specs=[pl.BlockSpec((1, share,...]
    all_gather x1 -> x0, blocking collectives: 21.8 us -> none  [local(): lax.all_gather(activations, 'hidden', axis=0, tiled=True)]
    reduce_sum x9 -> x1, other arithmetic: 15.3 us -> 0.02 us  [local(): gram = jnp.sum(gram, axis=0)]
    add x5 -> x0, other arithmetic: 10.8 us -> none  [the longest x4 9.97 us: blend(): return kept_coef * kept_half + came_coef * came_half]
  transfers between devices with their start and end apart: 5 -> 3, of which waited for: 5 -> 3; matrix products, arithmetic and copies ran while one was open for 0% -> 1% of each run, Pallas kernels for 0% -> 0%
where the time goes in v1:
time: 198 us; the launch traced here: 195 us
  blocking collectives  104 us (53%)
  Pallas kernels  51.4 us (26%)
  between operations  13.4 us (7%)
  starting transfers between devices  10.6 us (5%)
  waiting for transfers between devices  10.6 us (5%)
  local copies, waits for them, and re-layouts  3.93 us (2%)
    pallas_call x1, Pallas kernels, local(): pl.pallas_call(gram_kernel, grid=(NR,), in_specs=[pl.BlockSpec((1, share,...  39 us
    all_to_all x1, blocking collectives, local(): halves = lax.all_to_all(halves, ('x', 'z', 'core'), 0, 0, tiled=True)  29.3 us
    all_to_all x1, blocking collectives, local(): lax.all_to_all(grad_out.T.reshape(NR, share, TOK), XZ, 0, 0, tiled=True)  25.9 us
    all_to_all x1, blocking collectives, local(): lax.all_to_all(jnp.broadcast_to(gram, (16, 8, LANES)), ('z', 'core'), 0,...  16.6 us
    all_to_all x1, blocking collectives, local(): lax.all_to_all(jnp.broadcast_to(gram, (32, 8, LANES)), ('x', 'y'), 0, 0,...  15.9 us
    all_to_all x1, blocking collectives, local(): pieces = lax.all_to_all(pieces, XZ, 0, 0, tiled=True)  15.9 us
    pallas_call x1, Pallas kernels, local(): pl.pallas_call(combine_kernel, grid=(2 * share // block,), in_specs=[pl.B...  10.4 us
    all_gather x1, waiting for transfers between devices, local(): lax.all_gather(halves.reshape(NR * 16, depth), 'y', axis=0, tiled=True)  7.51 us
  transfers between devices with their start and end apart: 3, of which 3 were waited for; matrix products, arithmetic and copies ran while one was open for 1% of the time, Pallas kernels for 0%

profile of v1, /device:TPU:1, one launch (start us, length us, event | category | flops | bytes accessed | tf_op | source)
XLA Modules:
  0.0 194.6 jit_solution(13960115175145555520)
XLA Ops:
  6.5 0.0 all-gather.2.cloned.1.call-start
  6.5 0.7 broadcast_in_dim.12
  7.3 29.3 %all_to_all.25 = bf16[64,8,384]{2,1,0:T(8,128)(2,1)} all-to-all(bf16[64,8,384]{2,1,0:T(8,128)(2,1)S(1)} %bitcast.21), channel_id=1, replica_groups=mesh['x'=4,'z'=8,'y'=8,'core'=2] {'x','z','core'}, dimensions={0} | all-to-all | bytes 786432 | tf_op jit(solution)/shard_map/all_to_all | solution.py:151
  36.6 0.0 all-gather.2.cloned.1.call-update
  36.6 1.5 copy.5
  38.1 25.9 %all_to_all.26.own_ref = bf16[32,104,128]{2,1,0:T(8,128)(2,1)S(1)} all-to-all(bf16[32,104,128]{2,1,0:T(8,128)(2,1)S(1)} %bitcast.17), channel_id=1, replica_groups=mesh['x'=4,'z'=8,'y'=8,'core'=2] {'x','z'}, dimensions={0} | all-to-all | bytes 1703936 | tf_op jit(solution)/shard_map/all_to_all | solution.py:155
  64.1 0.0 copy-start
  64.1 6.6 %collective-permute-start = (bf16[32,104,128]{2,1,0:T(8,128)(2,1)S(1)}, bf16[32,104,128]{2,1,0:T(8,128)(2,1)S(1)}, u32[]{:S(2)}, u32[]{:S(2)}) collective-permute-start(bf16[32,104,128]{2,1,0:T(8,128)(2,1)S(1)} %all_to_all.26.own_ref), channel_id=1, source_target_pairs={{0,1},{1,0},{2,3},{3,2},{4,5},{5,4},{6,7},{7,6},{8,9},{9,8},{10,11... | collective-permute-start | bytes 2555912 | tf_op jit(solution)/shard_map/ppermute | solution.py:156
  70.7 2.0 %collective-permute-done.oth_ref = bf16[32,104,128]{2,1,0:T(8,128)(2,1)S(1)} collective-permute-done((bf16[32,104,128]{2,1,0:T(8,128)(2,1)S(1)}, bf16[32,104,128]{2,1,0:T(8,128)(2,1)S(1)}, u32[]{:S(2)}, u32[]{:S(2)}) %collective-permute-start) | collective-permute-done | bytes 852000 | tf_op jit(solution)/shard_map/ppermute | solution.py:156
  72.7 0.0 copy-start.1
  72.7 7.5 %all-gather.2.cloned.1.call-done = bf16[4096,384]{1,0:T(8,128)(2,1)} async-done(((bf16[512,384]{1,0:T(8,128)(2,1)}), bf16[4096,384]{1,0:T(8,128)(2,1)}) %all-gather.2.cloned.1.call-update) | async-done | bytes 3145744 | tf_op jit(solution)/shard_map/all_gather | solution.py:152
  80.2 0.0 copy-done
  80.2 0.0 copy-done.1
  80.2 39.0 %gram.1 = (f32[32,208,384]{2,1,0:T(8,128)}, f32[8,128]{1,0:T(8,128)}) custom-call(bf16[32,104,128]{2,1,0:T(8,128)(2,1)} %copy-done, bf16[32,104,128]{2,1,0:T(8,128)(2,1)} %copy-done.1, bf16[8,32,16,384]{3,2,1,0:T(8,128)(2,1)} %bitcast.18), custom_call_target="tpu_custom_call" | custom-call | tf_op jit(solution)/shard_map/gram/pallas_call | solution.py:158
  119.2 0.7 broadcast_in_dim.13
  119.9 16.6 %all_to_all.27 = f32[16,8,128]{2,1,0:T(8,128)S(1)} all-to-all(f32[16,8,128]{2,1,0:T(8,128)S(1)} %broadcast_in_dim.13), channel_id=1, replica_groups=mesh['x'=4,'z'=8,'y'=8,'core'=2] {'z','core'}, dimensions={0} | all-to-all | bytes 131072 | tf_op jit(solution)/shard_map/all_to_all | solution.py:181
  136.5 15.9 %all_to_all.28.part_ref = f32[32,8,128]{2,1,0:T(8,128)} all-to-all(f32[32,8,128]{2,1,0:T(8,128)S(1)} %broadcast_in_dim.14), channel_id=1, replica_groups=mesh['x'=4,'z'=8,'y'=8,'core'=2] {'x','y'}, dimensions={0} | all-to-all | bytes 262144 | tf_op jit(solution)/shard_map/all_to_all | solution.py:183
  152.5 10.4 %combine.1 = f32[2,384,128]{2,1,0:T(8,128)} custom-call(f32[32,8,128]{2,1,0:T(8,128)} %all_to_all.28.part_ref, f32[32,208,384]{2,1,0:T(8,128)} %get-tuple-element.8.g_ref), custom_call_target="tpu_custom_call" | custom-call | tf_op jit(solution)/shard_map/combine/pallas_call | solution.py:186
  162.8 0.9 slice_bitcast_fusion
  163.8 4.0 %collective-permute-start.1 = (f32[384,128]{1,0:T(8,128)S(1)}, f32[384,128]{1,0:T(8,128)S(1)}, u32[]{:S(2)}, u32[]{:S(2)}) collective-permute-start(f32[384,128]{1,0:T(8,128)S(1)} %slice_bitcast_fusion), channel_id=1, source_target_pairs={{0,1},{1,0},{2,3},{3,2},{4,5},{5,4},{6,7},{7,6},{8,9},{9,8},{10,11... | collective-permute-start | bytes 589832 | tf_op jit(solution)/shard_map/ppermute | solution.py:203
  167.8 1.0 collective-permute-done.1
  168.9 1.0 fusion.1
  169.9 15.9 %all_to_all.29.pieces_ref = f32[32,24,128]{2,1,0:T(8,128)} all-to-all(f32[32,24,128]{2,1,0:T(8,128)S(1)} %bitcast.20), channel_id=1, replica_groups=mesh['x'=4,'z'=8,'y'=8,'core'=2] {'x','z'}, dimensions={0} | all-to-all | bytes 786432 | tf_op jit(solution)/shard_map/all_to_all | solution.py:207
  185.7 2.0 %finish.1 = f32[24,3328]{1,0:T(8,128)} custom-call(f32[32,24,128]{2,1,0:T(8,128)} %all_to_all.29.pieces_ref, f32[24,3328]{1,0:T(8,128)} %momentum_ref.1), custom_call_target="tpu_custom_call" | custom-call | tf_op jit(solution)/shard_map/finish/pallas_call | solution.py:209
  (3 shorter events, 0.1 us)
Async XLA Ops:
  6.5 73.6 %all-gather.2.cloned.1.call-start = ((), (), s32[]{:S(2)}) async-start(), calls=%async_computation.5 | async-start | bytes 3538944 | tf_op jit(solution)/shard_map/all_gather | solution.py:152
  64.1 16.1 %copy-start = (bf16[32,104,128]{2,1,0:T(8,128)(2,1)}, bf16[32,104,128]{2,1,0:T(8,128)(2,1)S(1)}, u32[]{:S(2)}) copy-start(bf16[32,104,128]{2,1,0:T(8,128)(2,1)S(1)} %all_to_all.26.own_ref) | copy-start | bytes 2555908
  64.1 8.6 %collective-permute-start = (bf16[32,104,128]{2,1,0:T(8,128)(2,1)S(1)}, bf16[32,104,128]{2,1,0:T(8,128)(2,1)S(1)}, u32[]{:S(2)}, u32[]{:S(2)}) collective-permute-start(bf16[32,104,128]{2,1,0:T(8,128)(2,1)S(1)} %all_to_all.26.own_ref), channel_id=1, source_target_pairs={{0,1},{1,0},{2,3},{3,2},{4,5},{5,4},{6,7},{7,6},{8,9},{9,8},{10,11... | collective-permute-start | bytes 2555912 | tf_op jit(solution)/shard_map/ppermute | solution.py:156
  72.7 7.5 %copy-start.1 = (bf16[32,104,128]{2,1,0:T(8,128)(2,1)}, bf16[32,104,128]{2,1,0:T(8,128)(2,1)S(1)}, u32[]{:S(2)}) copy-start(bf16[32,104,128]{2,1,0:T(8,128)(2,1)S(1)} %collective-permute-done.oth_ref) | copy-start | bytes 2555908
  163.8 5.1 %collective-permute-start.1 = (f32[384,128]{1,0:T(8,128)S(1)}, f32[384,128]{1,0:T(8,128)S(1)}, u32[]{:S(2)}, u32[]{:S(2)}) collective-permute-start(f32[384,128]{1,0:T(8,128)S(1)} %slice_bitcast_fusion), channel_id=1, source_target_pairs={{0,1},{1,0},{2,3},{3,2},{4,5},{5,4},{6,7},{7,6},{8,9},{9,8},{10,11... | collective-permute-start | bytes 589832 | tf_op jit(solution)/shard_map/ppermute | solution.py:203
Sparse Core Ops, SparseCore 0:
  36.7 43.4 all-gather.1

commit v2 on v1

v2 whole, which is shorter than its diff:
```python
import functools

import jax
import jax.numpy as jnp
from jax import lax
from jax.experimental import pallas as pl
from jax.experimental.pallas import tpu as pltpu
from jax.sharding import Mesh, PartitionSpec as P

EPSILON = 1e-06
DECAY = 0.9
NR = 32
TOK = 128
LANES = 128
XZ = ("x", "z")
CORES = [(0, 1), (1, 0)]
CHUNKS = ((0, 384),)


def gram_kernel(cols_ref, *refs):
    act_refs, (g_out_ref, gram_ref, g_ref, q_ref, sem) = refs[:-5], refs[-5:]
    groups = cols_ref.shape[1] // 8
    depth = act_refs[0].shape[-1]
    lane_blocks = depth // LANES
    unroll = 26 // lane_blocks

    def one(r, carry):
        act = jnp.concatenate([ref[r] for ref in act_refs], axis=0)
        g_ref[r] = jnp.dot(cols_ref[r], act, preferred_element_type=jnp.float32)
        return carry

    lax.fori_loop(0, NR, one, 0, unroll=16)
    save = pltpu.make_async_copy(g_ref, g_out_ref, sem)
    save.start()
    q_ref[...] = jnp.zeros_like(q_ref)

    def pair_block(rb, sb):
        def body(f, acc):
            acc = list(acc)
            for h in range(unroll):
                row = pl.multiple_of((f * unroll + h) * 8, 8)
                for lb in range(lane_blocks):
                    lanes = slice(lb * LANES, (lb + 1) * LANES)
                    left = [g_ref[rb * 4 + i, pl.ds(row, 8), lanes] for i in range(4)]
                    right = [g_ref[sb * 4 + i, pl.ds(row, 8), lanes] for i in range(4)]
                    for i in range(4):
                        for j in range(4):
                            acc[i * 4 + j] = acc[i * 4 + j] + left[i] * right[j]
            return tuple(acc)

        zero = jnp.zeros((8, LANES), jnp.float32)
        acc = lax.fori_loop(0, groups // unroll, body, (zero,) * 16)
        for i in range(4):
            left_id = rb * 4 + i
            base = lax.rem(left_id, 8) * 128 + lax.div(left_id, 8) * 32
            for j in range(4):
                q_ref[pl.ds(base + sb * 4 + j, 1), :] = jnp.sum(
                    acc[i * 4 + j], axis=0, keepdims=True
                )

    def outer(rb, carry):
        def inner(sb, c):
            pair_block(rb, sb)
            return c

        return lax.fori_loop(rb, NR // 4, inner, carry)

    lax.fori_loop(0, NR // 4, outer, 0)
    sums = lax.dot_general(
        jnp.ones((8, LANES), jnp.float32),
        q_ref[...],
        (((1,), (1,)), ((), ())),
        precision=lax.Precision.HIGHEST,
        preferred_element_type=jnp.float32,
    )
    for i in range(8):
        gram_ref[i : i + 1, :] = sums[i : i + 1, i * LANES : (i + 1) * LANES]
    save.wait()


def tree_weights(packed):
    gram = jnp.concatenate([packed[:, 32 * q : 32 * q + 32] for q in range(4)], axis=0)
    rows = lax.broadcasted_iota(jnp.int32, (NR, NR), 0)
    cols = lax.broadcasted_iota(jnp.int32, (NR, NR), 1)
    upper = jnp.where(rows < cols, gram, 0.0)
    quad = jnp.where(rows == cols, gram, 2.0 * upper)
    w_col = jnp.ones((NR, 1), jnp.float32)
    w_row = jnp.ones((1, NR), jnp.float32)
    for level in range(5):
        scale = w_col * w_row
        same_half = (rows >> level) == (cols >> level)
        same_pair = (rows >> (level + 1)) == (cols >> (level + 1))
        squares = jnp.where(same_half, quad * scale, 0.0)
        crosses = jnp.where(same_pair & (~same_half), upper * scale, 0.0)

        def both(values, mask):
            down = jnp.sum(values, axis=1, keepdims=True)
            across = jnp.sum(values, axis=0, keepdims=True)
            as_row = jnp.sum(jnp.where(mask, down, 0.0), axis=0, keepdims=True)
            as_col = jnp.sum(jnp.where(mask, across, 0.0), axis=1, keepdims=True)
            return as_col, as_row

        sq_col, sq_row = both(squares, same_half)
        cr_col, cr_row = both(crosses, same_pair)
        w_col = w_col * (1.0 - cr_col / (2.0 * (sq_col + EPSILON)))
        w_row = w_row * (1.0 - cr_row / (2.0 * (sq_row + EPSILON)))
    return w_col


def combine_kernel(part_ref, *refs):
    n = len(CHUNKS)
    kept, (mine_ref, theirs_ref, w_ref, ct_ref) = refs[:n], refs[n : n + 4]
    g_refs, sem = refs[n + 4 : -1], refs[-1]
    share = g_refs[0].shape[1] // 2
    loads = [pltpu.make_async_copy(kept[k], g_refs[k], sem.at[k]) for k in range(n)]
    for load in loads:
        load.start()
    weights = tree_weights(jnp.sum(part_ref[...], axis=0))
    for r in range(NR):
        w_ref[r] = jnp.broadcast_to(weights[r : r + 1, :], (8, LANES))
    ct_ref[pl.ds(2 * share, 48), :] = jnp.zeros((48, ct_ref.shape[1]), jnp.float32)
    for load in loads:
        load.wait()
    blocks = [(g, lb) for g in g_refs for lb in range(g.shape[2] // LANES)]

    def body(f, carry):
        row = pl.multiple_of(f * 8, 8)
        acc = [None] * len(blocks)
        for r in range(NR):
            weight = w_ref[r]
            for k, (g, lb) in enumerate(blocks):
                term = g[r, pl.ds(row, 8), lb * LANES : (lb + 1) * LANES] * weight
                acc[k] = term if r == 0 else acc[k] + term
        for k in range(len(blocks)):
            ct_ref[pl.ds(row, 8), k * LANES : (k + 1) * LANES] = acc[k]
        return carry

    lax.fori_loop(0, 2 * share // 8, body, 0)
    for part, ref in enumerate((mine_ref, theirs_ref)):
        for k in range(len(blocks)):
            lanes = slice(k * LANES, (k + 1) * LANES)
            ref[lanes, :] = ct_ref[share * part : share * part + LANES, lanes].T


def finish_kernel(pieces_ref, momentum_ref, out_ref):
    width = momentum_ref.shape[1] // pieces_ref.shape[0]
    row = jnp.concatenate([pieces_ref[k][:, :width] for k in range(pieces_ref.shape[0])], axis=1)
    out_ref[...] = DECAY * momentum_ref[...] + row


def ring(block):
    size = lax.axis_size("y")
    up = [(i, (i + 1) % size) for i in range(size)]
    down = [(i, (i - 1) % size) for i in range(size)]
    above, below = [block], [block]
    for step in range(size // 2):
        below.append(lax.ppermute(below[-1], "y", up))
        if step < size // 2 - 1:
            above.append(lax.ppermute(above[-1], "y", down))
    return above + below[:0:-1]


def local(activations, grad_out, momentum):
    core = lax.axis_index("core")
    columns = grad_out.shape[1]
    share = columns // NR
    depth = activations.shape[1] // 2

    halves = activations.reshape(8, 2, depth).transpose(1, 0, 2)
    halves = jnp.broadcast_to(halves[None], (NR, 2, 8, depth)).reshape(2 * NR, 8, depth)
    halves = lax.all_to_all(halves, ("x", "z", "core"), 0, 0, tiled=True)
    halves = halves.reshape(NR * 16, depth)

    shift = 16 * lax.axis_index("y")
    rolled = lax.dynamic_slice_in_dim(jnp.concatenate([grad_out, grad_out], axis=0), shift, TOK, 0)
    own = lax.all_to_all(rolled.T.reshape(NR, share, TOK), XZ, 0, 0, tiled=True)
    other = lax.ppermute(own, "core", CORES)
    cols = jnp.concatenate([own, other], axis=1)

    grads, grams = [], []
    for start, width in CHUNKS:
        acts = ring(halves[:, start : start + width].reshape(NR, 16, width))
        grad, gram = pl.pallas_call(
            gram_kernel,
            out_shape=[
                jax.ShapeDtypeStruct((NR, 2 * share, width), jnp.float32),
                jax.ShapeDtypeStruct((8, LANES), jnp.float32),
            ],
            out_specs=[
                pl.BlockSpec(memory_space=pltpu.HBM),
                pl.BlockSpec(memory_space=pltpu.VMEM),
            ],
            scratch_shapes=[
                pltpu.VMEM((NR, 2 * share, width), jnp.float32),
                pltpu.VMEM((1024, LANES), jnp.float32),
                pltpu.SemaphoreType.DMA,
            ],
            compiler_params=pltpu.CompilerParams(vmem_limit_bytes=60 << 20),
            name="gram",
        )(cols, *acts)
        grads.append(grad)
        grams.append(gram)
    gram = sum(grams)

    gram = lax.all_to_all(jnp.broadcast_to(gram, (16, 8, LANES)), ("z", "core"), 0, 0, tiled=True)
    gram = jnp.sum(gram, axis=0)
    gram = lax.all_to_all(jnp.broadcast_to(gram, (32, 8, LANES)), ("x", "y"), 0, 0, tiled=True)

    mine, theirs = pl.pallas_call(
        combine_kernel,
        out_shape=[jax.ShapeDtypeStruct((depth, LANES), jnp.float32)] * 2,
        scratch_shapes=[
            pltpu.VMEM((NR, 8, LANES), jnp.float32),
            pltpu.VMEM((256, depth), jnp.float32),
            *(pltpu.VMEM(g.shape, jnp.float32) for g in grads),
            pltpu.SemaphoreType.DMA((len(grads),)),
        ],
        in_specs=[pl.BlockSpec(memory_space=pltpu.VMEM)]
        + [pl.BlockSpec(memory_space=pltpu.HBM)] * len(grads),
        compiler_params=pltpu.CompilerParams(vmem_limit_bytes=60 << 20),
        name="combine",
    )(gram, *grads)
    came = lax.ppermute(theirs, "core", CORES)
    low = jnp.where(core == 0, mine, came)
    high = jnp.where(core == 0, came, mine)
    pieces = jnp.concatenate([low, high], axis=0).reshape(NR, 24, LANES)
    pieces = lax.all_to_all(pieces, XZ, 0, 0, tiled=True)

    return pl.pallas_call(
        finish_kernel,
        out_shape=jax.ShapeDtypeStruct(momentum.shape, jnp.float32),
        compiler_params=pltpu.CompilerParams(vmem_limit_bytes=4 << 20),
        name="finish",
    )(pieces, momentum)


def solution(mesh):
    devices = mesh.devices.reshape(4, 8, 8, 2)
    fine = Mesh(devices, ("x", "z", "y", "core"))
    dp, hidden = ("x", "z"), ("y", "core")
    return jax.shard_map(
        local,
        mesh=fine,
        in_specs=(P(dp + hidden, None), P(dp, hidden), P(dp, hidden)),
        out_specs=P(dp, hidden),
        check_vma=False,
    )
```

time: 198 us -> 173 us (0.87)
  blocking collectives: 104 us -> 42 us
  starting transfers between devices: 10.6 us -> 53.9 us
  waiting for transfers between devices: 10.6 us -> 42.1 us
  Pallas kernels: 51.4 us -> 26 us
  between operations: 13.4 us -> 0.24 us
    all_to_all x2 -> x0, blocking collectives: 55.2 us -> none  [the longest x1 29.3 us: local(): halves = lax.all_to_all(halves, ('x', 'z', 'core'), 0, 0, tiled=True)]
    pallas_call x2, Pallas kernels: 49.4 us -> 25.1 us  [the longest x1 18.1 us: local(): pl.pallas_call(gram_kernel, out_shape=[jax.ShapeDtypeStruct((NR, 2 * shar...]
    ppermute x1 -> x8, starting transfers between devices: 4.02 us -> 27.3 us  [the longest x3 14.2 us: ring(): above.append(lax.ppermute(above[-1], 'y', down))]
    ppermute x1 -> x8, waiting for transfers between devices: 1.04 us -> 23.9 us  [the longest x4 11.8 us: ring(): below.append(lax.ppermute(below[-1], 'y', up))]
    all_to_all x0 -> x2, starting transfers between devices: none -> 20 us  [the longest x1 14.8 us: local(): halves = lax.all_to_all(halves, ('x', 'z', 'core'), 0, 0, tiled=True)]
    all_to_all x0 -> x2, waiting for transfers between devices: none -> 18.2 us  [the longest x1 12.9 us: local(): halves = lax.all_to_all(halves, ('x', 'z', 'core'), 0, 0, tiled=True)]
    all_gather x1 -> x0, waiting for transfers between devices: 7.51 us -> none  [local(): lax.all_gather(halves.reshape(NR * 16, depth), 'y', axis=0, tiled=True)]
    all_to_all x1, blocking collectives: 16.6 us -> 13.1 us  [local(): lax.all_to_all(jnp.broadcast_to(gram, (16, 8, LANES)), ('z', 'core'), 0,...]
  transfers between devices with their start and end apart: 3 -> 11, of which waited for: 3 -> 7; matrix products, arithmetic and copies ran while one was open for 1% -> 2% of each run, Pallas kernels for 0% -> 0%
where the time goes in v2:
time: 173 us; the launch traced here: 171 us
  starting transfers between devices  53.9 us (31%)
  waiting for transfers between devices  42.1 us (24%)
  blocking collectives  42 us (24%)
  Pallas kernels  26 us (15%)
  local copies, waits for them, and re-layouts  3.57 us (2%)
  other arithmetic  2.74 us (2%)
    pallas_call x1, Pallas kernels, local(): pl.pallas_call(gram_kernel, out_shape=[jax.ShapeDtypeStruct((NR, 2 * shar...  18.1 us
    all_to_all x1, starting transfers between devices, local(): halves = lax.all_to_all(halves, ('x', 'z', 'core'), 0, 0, tiled=True)  14.8 us
    all_to_all x1, blocking collectives, local(): pieces = lax.all_to_all(pieces, XZ, 0, 0, tiled=True)  14.8 us
    ppermute x3, starting transfers between devices, ring(): above.append(lax.ppermute(above[-1], 'y', down))  14.2 us
    all_to_all x1, blocking collectives, local(): lax.all_to_all(jnp.broadcast_to(gram, (32, 8, LANES)), ('x', 'y'), 0, 0,...  14.2 us
    all_to_all x1, blocking collectives, local(): lax.all_to_all(jnp.broadcast_to(gram, (16, 8, LANES)), ('z', 'core'), 0,...  13.1 us
    all_to_all x1, waiting for transfers between devices, local(): halves = lax.all_to_all(halves, ('x', 'z', 'core'), 0, 0, tiled=True)  12.9 us
    ppermute x4, waiting for transfers between devices, ring(): below.append(lax.ppermute(below[-1], 'y', up))  11.8 us
  transfers between devices with their start and end apart: 11, of which 7 were waited for; matrix products, arithmetic and copies ran while one was open for 2% of the time, Pallas kernels for 0%

profile of v2, /device:TPU:1, one launch (start us, length us, event | category | flops | bytes accessed | tf_op | source)
XLA Modules:
  0.0 170.6 jit_solution(18006949149874373067)
XLA Ops:
  0.0 1.6 broadcast_in_dim.12
  1.6 14.8 %all-to-all-start.1 = ((bf16[64,8,384]{2,1,0:T(8,128)(2,1)}), bf16[64,8,384]{2,1,0:T(8,128)(2,1)S(1)}, u32[]{:S(2)}, u32[]{:S(2)}) async-start(bf16[64,8,384]{2,1,0:T(8,128)(2,1)} %bitcast.4), calls=%async_computation.1 | async-start | bytes 786432 | tf_op jit(solution)/shard_map/all_to_all | solution.py:171
  18.1 12.9 %all-to-all-done.1 = bf16[64,8,384]{2,1,0:T(8,128)(2,1)S(1)} async-done(((bf16[64,8,384]{2,1,0:T(8,128)(2,1)}), bf16[64,8,384]{2,1,0:T(8,128)(2,1)S(1)}, u32[]{:S(2)}, u32[]{:S(2)}) %all-to-all-start.1) | async-done | bytes 393248 | tf_op jit(solution)/shard_map/all_to_all | solution.py:171
  31.0 5.2 %all-to-all-start = ((bf16[32,104,128]{2,1,0:T(8,128)(2,1)}), bf16[32,104,128]{2,1,0:T(8,128)(2,1)S(1)}, u32[]{:S(2)}, u32[]{:S(2)}) async-start(bf16[32,104,128]{2,1,0:T(8,128)(2,1)} %bitcast.1), calls=%async_computation | async-start | bytes 1703936 | tf_op jit(solution)/shard_map/all_to_all | solution.py:176
  36.2 3.2 %collective-permute-start.4 = (bf16[32,16,384]{2,1,0:T(8,128)(2,1)S(1)}, bf16[32,16,384]{2,1,0:T(8,128)(2,1)S(1)}, u32[]{:S(2)}, u32[]{:S(2)}) collective-permute-start(bf16[32,16,384]{2,1,0:T(8,128)(2,1)S(1)} %bitcast.9), channel_id=1, source_target_pairs={{0,2},{2,4},{4,6},{6,8},{8,10},{10,12},{12,14},{14,0},{1,3},{3,5},... | collective-permute-start | bytes 1179656 | tf_op jit(solution)/shard_map/ppermute | solution.py:157
  39.4 3.8 %collective-permute-start.1 = (bf16[32,16,384]{2,1,0:T(8,128)(2,1)S(1)}, bf16[32,16,384]{2,1,0:T(8,128)(2,1)S(1)}, u32[]{:S(2)}, u32[]{:S(2)}) collective-permute-start(bf16[32,16,384]{2,1,0:T(8,128)(2,1)S(1)} %bitcast.10), channel_id=1, source_target_pairs={{0,14},{2,0},{4,2},{6,4},{8,6},{10,8},{12,10},{14,12},{1,15},{3,1}... | collective-permute-start | bytes 1179656 | tf_op jit(solution)/shard_map/ppermute | solution.py:159
  43.2 6.7 %collective-permute-done.4.refs_7_ = bf16[32,16,384]{2,1,0:T(8,128)(2,1)S(1)} collective-permute-done((bf16[32,16,384]{2,1,0:T(8,128)(2,1)S(1)}, bf16[32,16,384]{2,1,0:T(8,128)(2,1)S(1)}, u32[]{:S(2)}, u32[]{:S(2)}) %collective-permute-start.4) | collective-permute-done | bytes 393248 | tf_op jit(solution)/shard_map/ppermute | solution.py:157
  49.9 1.9 %collective-permute-start.5 = (bf16[32,16,384]{2,1,0:T(8,128)(2,1)S(1)}, bf16[32,16,384]{2,1,0:T(8,128)(2,1)S(1)}, u32[]{:S(2)}, u32[]{:S(2)}) collective-permute-start(bf16[32,16,384]{2,1,0:T(8,128)(2,1)S(1)} %collective-permute-done.4.refs_7_), channel_id=1, source_target_pairs={{0,2},{2,4},{4,6},{6,8},{8,10},{10,12},{12,14},{14,0},{1,3},{3,5},... | collective-permute-start | bytes 1179656 | tf_op jit(solution)/shard_map/ppermute | solution.py:157
  51.8 5.3 %all-to-all-done = bf16[32,104,128]{2,1,0:T(8,128)(2,1)S(1)} async-done(((bf16[32,104,128]{2,1,0:T(8,128)(2,1)}), bf16[32,104,128]{2,1,0:T(8,128)(2,1)S(1)}, u32[]{:S(2)}, u32[]{:S(2)}) %all-to-all-start) | async-done | bytes 852000 | tf_op jit(solution)/shard_map/all_to_all | solution.py:176
  57.1 6.6 %collective-permute-start = (bf16[32,104,128]{2,1,0:T(8,128)(2,1)S(1)}, bf16[32,104,128]{2,1,0:T(8,128)(2,1)S(1)}, u32[]{:S(2)}, u32[]{:S(2)}) collective-permute-start(bf16[32,104,128]{2,1,0:T(8,128)(2,1)S(1)} %all-to-all-done), channel_id=1, source_target_pairs={{0,1},{1,0},{2,3},{3,2},{4,5},{5,4},{6,7},{7,6},{8,9},{9,8},{10,11... | collective-permute-start | bytes 2555912 | tf_op jit(solution)/shard_map/ppermute | solution.py:177
  63.7 5.1 %collective-permute-start.2 = (bf16[32,16,384]{2,1,0:T(8,128)(2,1)S(1)}, bf16[32,16,384]{2,1,0:T(8,128)(2,1)S(1)}, u32[]{:S(2)}, u32[]{:S(2)}) collective-permute-start(bf16[32,16,384]{2,1,0:T(8,128)(2,1)S(1)} %collective-permute-done.1.refs_1_), channel_id=1, source_target_pairs={{0,14},{2,0},{4,2},{6,4},{8,6},{10,8},{12,10},{14,12},{1,15},{3,1}... | collective-permute-start | bytes 1179656 | tf_op jit(solution)/shard_map/ppermute | solution.py:159
  68.9 1.9 %collective-permute-start.6 = (bf16[32,16,384]{2,1,0:T(8,128)(2,1)S(1)}, bf16[32,16,384]{2,1,0:T(8,128)(2,1)S(1)}, u32[]{:S(2)}, u32[]{:S(2)}) collective-permute-start(bf16[32,16,384]{2,1,0:T(8,128)(2,1)S(1)} %collective-permute-done.5.refs_6_), channel_id=1, source_target_pairs={{0,2},{2,4},{4,6},{6,8},{8,10},{10,12},{12,14},{14,0},{1,3},{3,5},... | collective-permute-start | bytes 1179656 | tf_op jit(solution)/shard_map/ppermute | solution.py:157
  70.8 6.5 %collective-permute-done.2.refs_2_ = bf16[32,16,384]{2,1,0:T(8,128)(2,1)S(1)} collective-permute-done((bf16[32,16,384]{2,1,0:T(8,128)(2,1)S(1)}, bf16[32,16,384]{2,1,0:T(8,128)(2,1)S(1)}, u32[]{:S(2)}, u32[]{:S(2)}) %collective-permute-start.2) | collective-permute-done | bytes 393248 | tf_op jit(solution)/shard_map/ppermute | solution.py:159
  77.3 5.3 %collective-permute-start.3 = (bf16[32,16,384]{2,1,0:T(8,128)(2,1)S(1)}, bf16[32,16,384]{2,1,0:T(8,128)(2,1)S(1)}, u32[]{:S(2)}, u32[]{:S(2)}) collective-permute-start(bf16[32,16,384]{2,1,0:T(8,128)(2,1)S(1)} %collective-permute-done.2.refs_2_), channel_id=1, source_target_pairs={{0,14},{2,0},{4,2},{6,4},{8,6},{10,8},{12,10},{14,12},{1,15},{3,1}... | collective-permute-start | bytes 1179656 | tf_op jit(solution)/shard_map/ppermute | solution.py:159
  82.6 1.9 %collective-permute-start.7 = (bf16[32,16,384]{2,1,0:T(8,128)(2,1)S(1)}, bf16[32,16,384]{2,1,0:T(8,128)(2,1)}, u32[]{:S(2)}, u32[]{:S(2)}) collective-permute-start(bf16[32,16,384]{2,1,0:T(8,128)(2,1)S(1)} %collective-permute-done.6.refs_5_), channel_id=1, source_target_pairs={{0,2},{2,4},{4,6},{6,8},{8,10},{10,12},{12,14},{14,0},{1,3},{3,5},... | collective-permute-start | bytes 1179656 | tf_op jit(solution)/shard_map/ppermute | solution.py:157
  84.6 1.3 pad_maximum_fusion.cols_ref
  85.9 4.3 %collective-permute-done.3.refs_3_ = bf16[32,16,384]{2,1,0:T(8,128)(2,1)S(1)} collective-permute-done((bf16[32,16,384]{2,1,0:T(8,128)(2,1)S(1)}, bf16[32,16,384]{2,1,0:T(8,128)(2,1)S(1)}, u32[]{:S(2)}, u32[]{:S(2)}) %collective-permute-start.3) | collective-permute-done | bytes 393248 | tf_op jit(solution)/shard_map/ppermute | solution.py:159
  90.2 5.2 %collective-permute-done.7.refs_4_ = bf16[32,16,384]{2,1,0:T(8,128)(2,1)} collective-permute-done((bf16[32,16,384]{2,1,0:T(8,128)(2,1)S(1)}, bf16[32,16,384]{2,1,0:T(8,128)(2,1)}, u32[]{:S(2)}, u32[]{:S(2)}) %collective-permute-start.7) | collective-permute-done | bytes 393248 | tf_op jit(solution)/shard_map/ppermute | solution.py:157
  95.4 18.1 %gram.1 = (f32[32,208,384]{2,1,0:T(8,128)}, f32[8,128]{1,0:T(8,128)}) custom-call(bf16[32,208,128]{2,1,0:T(8,128)(2,1)} %pad_maximum_fusion.cols_ref, bf16[32,16,384]{2,1,0:T(8,128)(2,1)} %bitcast.11, bf16[32,16,384]{2,1,0:T(8,128)(2,1)} %copy-done.4, bf16[32,16,384]{2,1,0:T(8,128)(2,1)} %copy-done.6, bf16[32,16,384]{2,1,0:T(8,128)(2,1)} %copy-done.8, ...), custom_call_target="tpu_custom_call" | custom-call | tf_op jit(solution)/shard_map/gram/pallas_call | solution.py:183
  114.2 13.1 %all_to_all.25 = f32[16,8,128]{2,1,0:T(8,128)S(1)} all-to-all(f32[16,8,128]{2,1,0:T(8,128)S(1)} %broadcast_in_dim.13), channel_id=1, replica_groups=mesh['x'=4,'z'=8,'y'=8,'core'=2] {'z','core'}, dimensions={0} | all-to-all | bytes 131072 | tf_op jit(solution)/shard_map/all_to_all | solution.py:205
  127.3 14.2 %all_to_all.26.part_ref = f32[32,8,128]{2,1,0:T(8,128)} all-to-all(f32[32,8,128]{2,1,0:T(8,128)S(1)} %broadcast_in_dim.14), channel_id=1, replica_groups=mesh['x'=4,'z'=8,'y'=8,'core'=2] {'x','y'}, dimensions={0} | all-to-all | bytes 262144 | tf_op jit(solution)/shard_map/all_to_all | solution.py:207
  141.5 7.0 %combine.1 = (f32[384,128]{1,0:T(8,128)}, f32[384,128]{1,0:T(8,128)}) custom-call(f32[32,8,128]{2,1,0:T(8,128)} %all_to_all.26.part_ref, f32[32,208,384]{2,1,0:T(8,128)} %get-tuple-element.10.refs_0_), custom_call_target="tpu_custom_call" | custom-call | tf_op jit(solution)/shard_map/combine/pallas_call | solution.py:209
  148.5 4.1 %collective-permute-start.8 = (f32[384,128]{1,0:T(8,128)}, f32[384,128]{1,0:T(8,128)S(1)}, u32[]{:S(2)}, u32[]{:S(2)}) collective-permute-start(f32[384,128]{1,0:T(8,128)} %get-tuple-element.12), channel_id=1, source_target_pairs={{0,1},{1,0},{2,3},{3,2},{4,5},{5,4},{6,7},{7,6},{8,9},{9,8},{10,11... | collective-permute-start | bytes 589832 | tf_op jit(solution)/shard_map/ppermute | solution.py:223
  154.9 14.8 %all_to_all.27.pieces_ref = f32[32,24,128]{2,1,0:T(8,128)S(1)} all-to-all(f32[32,24,128]{2,1,0:T(8,128)S(1)} %bitcast.12), channel_id=1, replica_groups=mesh['x'=4,'z'=8,'y'=8,'core'=2] {'x','z'}, dimensions={0} | all-to-all | bytes 786432 | tf_op jit(solution)/shard_map/all_to_all | solution.py:227
  (31 shorter events, 5.6 us)
Async XLA Ops:
  0.0 16.4 %copy-start.2 = (bf16[128,3328]{1,0:T(8,128)(2,1)S(1)}, bf16[128,3328]{1,0:T(8,128)(2,1)}, u32[]{:S(2)}) copy-start(bf16[128,3328]{1,0:T(8,128)(2,1)} %param.4) | copy-start | bytes 2555908
  1.6 29.4 %all-to-all-start.1 = ((bf16[64,8,384]{2,1,0:T(8,128)(2,1)}), bf16[64,8,384]{2,1,0:T(8,128)(2,1)S(1)}, u32[]{:S(2)}, u32[]{:S(2)}) async-start(bf16[64,8,384]{2,1,0:T(8,128)(2,1)} %bitcast.4), calls=%async_computation.1 | async-start | bytes 786432 | tf_op jit(solution)/shard_map/all_to_all | solution.py:171
  31.0 54.9 %copy-start.1 = (bf16[64,8,384]{2,1,0:T(8,128)(2,1)}, bf16[64,8,384]{2,1,0:T(8,128)(2,1)S(1)}, u32[]{:S(2)}) copy-start(bf16[64,8,384]{2,1,0:T(8,128)(2,1)S(1)} %all-to-all-done.1) | copy-start | bytes 1179652
  31.0 26.1 %all-to-all-start = ((bf16[32,104,128]{2,1,0:T(8,128)(2,1)}), bf16[32,104,128]{2,1,0:T(8,128)(2,1)S(1)}, u32[]{:S(2)}, u32[]{:S(2)}) async-start(bf16[32,104,128]{2,1,0:T(8,128)(2,1)} %bitcast.1), calls=%async_computation | async-start | bytes 1703936 | tf_op jit(solution)/shard_map/all_to_all | solution.py:176
  36.2 13.7 %collective-permute-start.4 = (bf16[32,16,384]{2,1,0:T(8,128)(2,1)S(1)}, bf16[32,16,384]{2,1,0:T(8,128)(2,1)S(1)}, u32[]{:S(2)}, u32[]{:S(2)}) collective-permute-start(bf16[32,16,384]{2,1,0:T(8,128)(2,1)S(1)} %bitcast.9), channel_id=1, source_target_pairs={{0,2},{2,4},{4,6},{6,8},{8,10},{10,12},{12,14},{14,0},{1,3},{3,5},... | collective-permute-start | bytes 1179656 | tf_op jit(solution)/shard_map/ppermute | solution.py:157
  39.4 24.3 %collective-permute-start.1 = (bf16[32,16,384]{2,1,0:T(8,128)(2,1)S(1)}, bf16[32,16,384]{2,1,0:T(8,128)(2,1)S(1)}, u32[]{:S(2)}, u32[]{:S(2)}) collective-permute-start(bf16[32,16,384]{2,1,0:T(8,128)(2,1)S(1)} %bitcast.10), channel_id=1, source_target_pairs={{0,14},{2,0},{4,2},{6,4},{8,6},{10,8},{12,10},{14,12},{1,15},{3,1}... | collective-permute-start | bytes 1179656 | tf_op jit(solution)/shard_map/ppermute | solution.py:159
  49.9 45.5 %copy-start.3 = (bf16[32,16,384]{2,1,0:T(8,128)(2,1)}, bf16[32,16,384]{2,1,0:T(8,128)(2,1)S(1)}, u32[]{:S(2)}) copy-start(bf16[32,16,384]{2,1,0:T(8,128)(2,1)S(1)} %collective-permute-done.4.refs_7_) | copy-start | bytes 1179652
  49.9 19.0 %collective-permute-start.5 = (bf16[32,16,384]{2,1,0:T(8,128)(2,1)S(1)}, bf16[32,16,384]{2,1,0:T(8,128)(2,1)S(1)}, u32[]{:S(2)}, u32[]{:S(2)}) collective-permute-start(bf16[32,16,384]{2,1,0:T(8,128)(2,1)S(1)} %collective-permute-done.4.refs_7_), channel_id=1, source_target_pairs={{0,2},{2,4},{4,6},{6,8},{8,10},{10,12},{12,14},{14,0},{1,3},{3,5},... | collective-permute-start | bytes 1179656 | tf_op jit(solution)/shard_map/ppermute | solution.py:157
  57.1 27.4 %collective-permute-start = (bf16[32,104,128]{2,1,0:T(8,128)(2,1)S(1)}, bf16[32,104,128]{2,1,0:T(8,128)(2,1)S(1)}, u32[]{:S(2)}, u32[]{:S(2)}) collective-permute-start(bf16[32,104,128]{2,1,0:T(8,128)(2,1)S(1)} %all-to-all-done), channel_id=1, source_target_pairs={{0,1},{1,0},{2,3},{3,2},{4,5},{5,4},{6,7},{7,6},{8,9},{9,8},{10,11... | collective-permute-start | bytes 2555912 | tf_op jit(solution)/shard_map/ppermute | solution.py:177
  63.7 31.6 %copy-start.4 = (bf16[32,16,384]{2,1,0:T(8,128)(2,1)}, bf16[32,16,384]{2,1,0:T(8,128)(2,1)S(1)}, u32[]{:S(2)}) copy-start(bf16[32,16,384]{2,1,0:T(8,128)(2,1)S(1)} %collective-permute-done.1.refs_1_) | copy-start | bytes 1179652
  63.7 13.5 %collective-permute-start.2 = (bf16[32,16,384]{2,1,0:T(8,128)(2,1)S(1)}, bf16[32,16,384]{2,1,0:T(8,128)(2,1)S(1)}, u32[]{:S(2)}, u32[]{:S(2)}) collective-permute-start(bf16[32,16,384]{2,1,0:T(8,128)(2,1)S(1)} %collective-permute-done.1.refs_1_), channel_id=1, source_target_pairs={{0,14},{2,0},{4,2},{6,4},{8,6},{10,8},{12,10},{14,12},{1,15},{3,1}... | collective-permute-start | bytes 1179656 | tf_op jit(solution)/shard_map/ppermute | solution.py:159
  68.9 26.5 %copy-start.5 = (bf16[32,16,384]{2,1,0:T(8,128)(2,1)}, bf16[32,16,384]{2,1,0:T(8,128)(2,1)S(1)}, u32[]{:S(2)}) copy-start(bf16[32,16,384]{2,1,0:T(8,128)(2,1)S(1)} %collective-permute-done.5.refs_6_) | copy-start | bytes 1179652
  68.9 13.7 %collective-permute-start.6 = (bf16[32,16,384]{2,1,0:T(8,128)(2,1)S(1)}, bf16[32,16,384]{2,1,0:T(8,128)(2,1)S(1)}, u32[]{:S(2)}, u32[]{:S(2)}) collective-permute-start(bf16[32,16,384]{2,1,0:T(8,128)(2,1)S(1)} %collective-permute-done.5.refs_6_), channel_id=1, source_target_pairs={{0,2},{2,4},{4,6},{6,8},{8,10},{10,12},{12,14},{14,0},{1,3},{3,5},... | collective-permute-start | bytes 1179656 | tf_op jit(solution)/shard_map/ppermute | solution.py:157
  77.3 18.1 %copy-start.6 = (bf16[32,16,384]{2,1,0:T(8,128)(2,1)}, bf16[32,16,384]{2,1,0:T(8,128)(2,1)S(1)}, u32[]{:S(2)}) copy-start(bf16[32,16,384]{2,1,0:T(8,128)(2,1)S(1)} %collective-permute-done.2.refs_2_) | copy-start | bytes 1179652
  77.3 12.9 %collective-permute-start.3 = (bf16[32,16,384]{2,1,0:T(8,128)(2,1)S(1)}, bf16[32,16,384]{2,1,0:T(8,128)(2,1)S(1)}, u32[]{:S(2)}, u32[]{:S(2)}) collective-permute-start(bf16[32,16,384]{2,1,0:T(8,128)(2,1)S(1)} %collective-permute-done.2.refs_2_), channel_id=1, source_target_pairs={{0,14},{2,0},{4,2},{6,4},{8,6},{10,8},{12,10},{14,12},{1,15},{3,1}... | collective-permute-start | bytes 1179656 | tf_op jit(solution)/shard_map/ppermute | solution.py:159
  82.6 12.8 %copy-start.7 = (bf16[32,16,384]{2,1,0:T(8,128)(2,1)}, bf16[32,16,384]{2,1,0:T(8,128)(2,1)S(1)}, u32[]{:S(2)}) copy-start(bf16[32,16,384]{2,1,0:T(8,128)(2,1)S(1)} %collective-permute-done.6.refs_5_) | copy-start | bytes 1179652
  82.6 12.7 %collective-permute-start.7 = (bf16[32,16,384]{2,1,0:T(8,128)(2,1)S(1)}, bf16[32,16,384]{2,1,0:T(8,128)(2,1)}, u32[]{:S(2)}, u32[]{:S(2)}) collective-permute-start(bf16[32,16,384]{2,1,0:T(8,128)(2,1)S(1)} %collective-permute-done.6.refs_5_), channel_id=1, source_target_pairs={{0,2},{2,4},{4,6},{6,8},{8,10},{10,12},{12,14},{14,0},{1,3},{3,5},... | collective-permute-start | bytes 1179656 | tf_op jit(solution)/shard_map/ppermute | solution.py:157
  90.2 5.2 %copy-start.8 = (bf16[32,16,384]{2,1,0:T(8,128)(2,1)}, bf16[32,16,384]{2,1,0:T(8,128)(2,1)S(1)}, u32[]{:S(2)}) copy-start(bf16[32,16,384]{2,1,0:T(8,128)(2,1)S(1)} %collective-permute-done.3.refs_3_) | copy-start | bytes 1179652
  148.5 21.2 %copy-start = (f32[24,3328]{1,0:T(8,128)S(1)}, f32[24,3328]{1,0:T(8,128)}, u32[]{:S(2)}) copy-start(f32[24,3328]{1,0:T(8,128)} %momentum_ref.1) | copy-start | bytes 958468
  148.5 5.4 %collective-permute-start.8 = (f32[384,128]{1,0:T(8,128)}, f32[384,128]{1,0:T(8,128)S(1)}, u32[]{:S(2)}, u32[]{:S(2)}) collective-permute-start(f32[384,128]{1,0:T(8,128)} %get-tuple-element.12), channel_id=1, source_target_pairs={{0,1},{1,0},{2,3},{3,2},{4,5},{5,4},{6,7},{7,6},{8,9},{9,8},{10,11... | collective-permute-start | bytes 589832 | tf_op jit(solution)/shard_map/ppermute | solution.py:223

commit v3 on v2

--- a/solution.py
+++ b/solution.py
@@ -14,7 +14,7 @@
 LANES = 128
 XZ = ("x", "z")
 CORES = [(0, 1), (1, 0)]
-CHUNKS = ((0, 384),)
+CHUNKS = ((0, 256), (256, 128))
 
 
 def gram_kernel(cols_ref, *refs):
@@ -22,7 +22,8 @@
     groups = cols_ref.shape[1] // 8
     depth = act_refs[0].shape[-1]
     lane_blocks = depth // LANES
-    unroll = 26 // lane_blocks
+    unroll = 26 if lane_blocks == 1 else 13
+    assert groups % unroll == 0
 
     def one(r, carry):
         act = jnp.concatenate([ref[r] for ref in act_refs], axis=0)

time: 173 us -> 203 us (1.17)
  starting transfers between devices: 53.9 us -> 75.8 us
  Pallas kernels: 26 us -> 30.3 us
  blocking collectives: 42 us -> 45.1 us
    ppermute x3 -> x6, starting transfers between devices: 14.2 us -> 28.4 us  [ring(): above.append(lax.ppermute(above[-1], 'y', down))]
    all_to_all x1, waiting for transfers between devices: 5.32 us -> 17.7 us  [local(): own = lax.all_to_all(rolled.T.reshape(NR, share, TOK), XZ, 0, 0, tiled=True)]
    ppermute x3 -> x6, waiting for transfers between devices: 10.8 us -> 1.08 us  [ring(): above.append(lax.ppermute(above[-1], 'y', down))]
    ppermute x4 -> x8, starting transfers between devices: 8.96 us -> 16.6 us  [ring(): below.append(lax.ppermute(below[-1], 'y', up))]
    pallas_call x1 -> x2, Pallas kernels: 18.1 us -> 22.4 us  [local(): pl.pallas_call(gram_kernel, out_shape=[jax.ShapeDtypeStruct((NR, 2 * shar...]
    all_to_all x1, blocking collectives: 13.1 us -> 16.2 us  [local(): lax.all_to_all(jnp.broadcast_to(gram, (16, 8, LANES)), ('z', 'core'), 0,...]
    ppermute x4 -> x8, waiting for transfers between devices: 11.8 us -> 9.51 us  [ring(): below.append(lax.ppermute(below[-1], 'y', up))]
  transfers between devices with their start and end apart: 11 -> 18, of which waited for: 7 -> 6; matrix products, arithmetic and copies ran while one was open for 2% -> 1% of each run, Pallas kernels for 0% -> 7%
where the time goes in v3:
time: 203 us; the launch traced here: 200 us
  starting transfers between devices  75.8 us (37%)
  blocking collectives  45.1 us (22%)
  waiting for transfers between devices  42.4 us (21%)
  Pallas kernels  30.3 us (15%)
  local copies, waits for them, and re-layouts  3.88 us (2%)
  other arithmetic  2.12 us (1%)
    ppermute x6, starting transfers between devices, ring(): above.append(lax.ppermute(above[-1], 'y', down))  28.4 us
    pallas_call x2, Pallas kernels, local(): pl.pallas_call(gram_kernel, out_shape=[jax.ShapeDtypeStruct((NR, 2 * shar...  22.4 us
    all_to_all x1, waiting for transfers between devices, local(): own = lax.all_to_all(rolled.T.reshape(NR, share, TOK), XZ, 0, 0, tiled=True)  17.7 us
    ppermute x8, starting transfers between devices, ring(): below.append(lax.ppermute(below[-1], 'y', up))  16.6 us
    all_to_all x1, blocking collectives, local(): lax.all_to_all(jnp.broadcast_to(gram, (16, 8, LANES)), ('z', 'core'), 0,...  16.2 us
    all_to_all x1, starting transfers between devices, local(): halves = lax.all_to_all(halves, ('x', 'z', 'core'), 0, 0, tiled=True)  14.8 us
    all_to_all x1, blocking collectives, local(): pieces = lax.all_to_all(pieces, XZ, 0, 0, tiled=True)  14.8 us
    all_to_all x1, blocking collectives, local(): lax.all_to_all(jnp.broadcast_to(gram, (32, 8, LANES)), ('x', 'y'), 0, 0,...  14.2 us
  transfers between devices with their start and end apart: 18, of which 6 were waited for; matrix products, arithmetic and copies ran while one was open for 1% of the time, Pallas kernels for 7%

profile of v3, /device:TPU:1, one launch (start us, length us, event | category | flops | bytes accessed | tf_op | source)
XLA Modules:
  0.0 200.2 jit_solution(7814452831663457070)
XLA Ops:
  1.6 14.8 %all-to-all-start.1 = ((bf16[64,8,384]{2,1,0:T(8,128)(2,1)}), bf16[64,8,384]{2,1,0:T(8,128)(2,1)S(1)}, u32[]{:S(2)}, u32[]{:S(2)}) async-start(bf16[64,8,384]{2,1,0:T(8,128)(2,1)} %bitcast.4), calls=%async_computation.1 | async-start | bytes 786432 | tf_op jit(solution)/shard_map/all_to_all | solution.py:172
  18.1 12.8 %all-to-all-done.1 = bf16[64,8,384]{2,1,0:T(8,128)(2,1)S(1)} async-done(((bf16[64,8,384]{2,1,0:T(8,128)(2,1)}), bf16[64,8,384]{2,1,0:T(8,128)(2,1)S(1)}, u32[]{:S(2)}, u32[]{:S(2)}) %all-to-all-start.1) | async-done | bytes 393248 | tf_op jit(solution)/shard_map/all_to_all | solution.py:172
  31.0 5.2 %all-to-all-start = ((bf16[32,104,128]{2,1,0:T(8,128)(2,1)}), bf16[32,104,128]{2,1,0:T(8,128)(2,1)S(1)}, u32[]{:S(2)}, u32[]{:S(2)}) async-start(bf16[32,104,128]{2,1,0:T(8,128)(2,1)} %bitcast.1), calls=%async_computation | async-start | bytes 1703936 | tf_op jit(solution)/shard_map/all_to_all | solution.py:177
  36.2 3.2 %collective-permute-start.4 = (bf16[32,16,256]{2,1,0:T(8,128)(2,1)S(1)}, bf16[32,16,256]{2,1,0:T(8,128)(2,1)S(1)}, u32[]{:S(2)}, u32[]{:S(2)}) collective-permute-start(bf16[32,16,256]{2,1,0:T(8,128)(2,1)S(1)} %bitcast.14), channel_id=1, source_target_pairs={{0,2},{2,4},{4,6},{6,8},{8,10},{10,12},{12,14},{14,0},{1,3},{3,5},... | collective-permute-start | bytes 786440 | tf_op jit(solution)/shard_map/ppermute | solution.py:158
  39.4 17.7 %all-to-all-done = bf16[32,104,128]{2,1,0:T(8,128)(2,1)S(1)} async-done(((bf16[32,104,128]{2,1,0:T(8,128)(2,1)}), bf16[32,104,128]{2,1,0:T(8,128)(2,1)S(1)}, u32[]{:S(2)}, u32[]{:S(2)}) %all-to-all-start) | async-done | bytes 852000 | tf_op jit(solution)/shard_map/all_to_all | solution.py:177
  57.1 6.6 %collective-permute-start = (bf16[32,104,128]{2,1,0:T(8,128)(2,1)S(1)}, bf16[32,104,128]{2,1,0:T(8,128)(2,1)S(1)}, u32[]{:S(2)}, u32[]{:S(2)}) collective-permute-start(bf16[32,104,128]{2,1,0:T(8,128)(2,1)S(1)} %all-to-all-done), channel_id=1, source_target_pairs={{0,1},{1,0},{2,3},{3,2},{4,5},{5,4},{6,7},{7,6},{8,9},{9,8},{10,11... | collective-permute-start | bytes 2555912 | tf_op jit(solution)/shard_map/ppermute | solution.py:178
  63.7 5.1 %collective-permute-start.1 = (bf16[32,16,256]{2,1,0:T(8,128)(2,1)S(1)}, bf16[32,16,256]{2,1,0:T(8,128)(2,1)S(1)}, u32[]{:S(2)}, u32[]{:S(2)}) collective-permute-start(bf16[32,16,256]{2,1,0:T(8,128)(2,1)S(1)} %bitcast.15), channel_id=1, source_target_pairs={{0,14},{2,0},{4,2},{6,4},{8,6},{10,8},{12,10},{14,12},{1,15},{3,1}... | collective-permute-start | bytes 786440 | tf_op jit(solution)/shard_map/ppermute | solution.py:160
  68.8 1.9 collective-permute-start.5
  72.7 4.6 %collective-permute-start.8 = (bf16[32,16,128]{2,1,0:T(8,128)(2,1)S(1)}, bf16[32,16,128]{2,1,0:T(8,128)(2,1)S(1)}, u32[]{:S(2)}, u32[]{:S(2)}) collective-permute-start(bf16[32,16,128]{2,1,0:T(8,128)(2,1)S(1)} %bitcast.18), channel_id=1, source_target_pairs={{0,14},{2,0},{4,2},{6,4},{8,6},{10,8},{12,10},{14,12},{1,15},{3,1}... | collective-permute-start | bytes 393224 | tf_op jit(solution)/shard_map/ppermute | solution.py:160
  77.3 5.0 %collective-permute-done.11.refs_7_ = bf16[32,16,128]{2,1,0:T(8,128)(2,1)S(1)} collective-permute-done((bf16[32,16,128]{2,1,0:T(8,128)(2,1)S(1)}, bf16[32,16,128]{2,1,0:T(8,128)(2,1)S(1)}, u32[]{:S(2)}, u32[]{:S(2)}) %collective-permute-start.11) | collective-permute-done | bytes 131104 | tf_op jit(solution)/shard_map/ppermute | solution.py:158
  84.3 4.6 %collective-permute-start.2 = (bf16[32,16,256]{2,1,0:T(8,128)(2,1)S(1)}, bf16[32,16,256]{2,1,0:T(8,128)(2,1)S(1)}, u32[]{:S(2)}, u32[]{:S(2)}) collective-permute-start(bf16[32,16,256]{2,1,0:T(8,128)(2,1)S(1)} %collective-permute-done.1.refs_1_), channel_id=1, source_target_pairs={{0,14},{2,0},{4,2},{6,4},{8,6},{10,8},{12,10},{14,12},{1,15},{3,1}... | collective-permute-start | bytes 786440 | tf_op jit(solution)/shard_map/ppermute | solution.py:160
  90.8 4.6 %collective-permute-start.9 = (bf16[32,16,128]{2,1,0:T(8,128)(2,1)S(1)}, bf16[32,16,128]{2,1,0:T(8,128)(2,1)}, u32[]{:S(2)}, u32[]{:S(2)}) collective-permute-start(bf16[32,16,128]{2,1,0:T(8,128)(2,1)S(1)} %collective-permute-done.8.refs_1_), channel_id=1, source_target_pairs={{0,14},{2,0},{4,2},{6,4},{8,6},{10,8},{12,10},{14,12},{1,15},{3,1}... | collective-permute-start | bytes 393224 | tf_op jit(solution)/shard_map/ppermute | solution.py:160
  95.4 1.9 collective-permute-start.13
  97.4 5.0 %collective-permute-start.10 = (bf16[32,16,128]{2,1,0:T(8,128)(2,1)}, bf16[32,16,128]{2,1,0:T(8,128)(2,1)}, u32[]{:S(2)}, u32[]{:S(2)}) collective-permute-start(bf16[32,16,128]{2,1,0:T(8,128)(2,1)} %collective-permute-done.9.refs_2_), channel_id=1, source_target_pairs={{0,14},{2,0},{4,2},{6,4},{8,6},{10,8},{12,10},{14,12},{1,15},{3,1}... | collective-permute-start | bytes 393224 | tf_op jit(solution)/shard_map/ppermute | solution.py:160
  104.4 4.6 %collective-permute-start.3 = (bf16[32,16,256]{2,1,0:T(8,128)(2,1)S(1)}, bf16[32,16,256]{2,1,0:T(8,128)(2,1)S(1)}, u32[]{:S(2)}, u32[]{:S(2)}) collective-permute-start(bf16[32,16,256]{2,1,0:T(8,128)(2,1)S(1)} %collective-permute-done.2.refs_2_), channel_id=1, source_target_pairs={{0,14},{2,0},{4,2},{6,4},{8,6},{10,8},{12,10},{14,12},{1,15},{3,1}... | collective-permute-start | bytes 786440 | tf_op jit(solution)/shard_map/ppermute | solution.py:160
  109.0 1.9 collective-permute-start.7
  113.0 4.4 %collective-permute-done.7.refs_4_ = bf16[32,16,256]{2,1,0:T(8,128)(2,1)} collective-permute-done((bf16[32,16,256]{2,1,0:T(8,128)(2,1)S(1)}, bf16[32,16,256]{2,1,0:T(8,128)(2,1)}, u32[]{:S(2)}, u32[]{:S(2)}) %collective-permute-start.7) | collective-permute-done | bytes 262176 | tf_op jit(solution)/shard_map/ppermute | solution.py:158
  117.5 13.6 %gram.2 = (f32[32,208,256]{2,1,0:T(8,128)}, f32[8,128]{1,0:T(8,128)}) custom-call(bf16[32,208,128]{2,1,0:T(8,128)(2,1)} %copy-done.1, bf16[32,16,256]{2,1,0:T(8,128)(2,1)} %bitcast.16, bf16[32,16,256]{2,1,0:T(8,128)(2,1)} %copy-done.6, bf16[32,16,256]{2,1,0:T(8,128)(2,1)} %copy-done.8, bf16[32,16,256]{2,1,0:T(8,128)(2,1)} %copy-done.10, ...), custom_call_target="tpu_custom_call" | custom-call | tf_op jit(solution)/shard_map/gram/pallas_call | solution.py:184
  131.1 8.8 %gram.3 = (f32[32,208,128]{2,1,0:T(8,128)}, f32[8,128]{1,0:T(8,128)}) custom-call(bf16[32,208,128]{2,1,0:T(8,128)(2,1)} %copy-done.1, bf16[32,16,128]{2,1,0:T(8,128)(2,1)} %bitcast.19, bf16[32,16,128]{2,1,0:T(8,128)(2,1)} %copy-done.12, bf16[32,16,128]{2,1,0:T(8,128)(2,1)} %collective-permute-done.9.refs_2_, ...), custom_call_target="tpu_custom_call" | custom-call | tf_op jit(solution)/shard_map/gram/pallas_call | solution.py:184
  140.6 16.2 %all_to_all.25 = f32[16,8,128]{2,1,0:T(8,128)S(1)} all-to-all(f32[16,8,128]{2,1,0:T(8,128)S(1)} %broadcast_in_dim.13), channel_id=1, replica_groups=mesh['x'=4,'z'=8,'y'=8,'core'=2] {'z','core'}, dimensions={0} | all-to-all | bytes 131072 | tf_op jit(solution)/shard_map/all_to_all | solution.py:206
  156.8 14.2 %all_to_all.26.part_ref = f32[32,8,128]{2,1,0:T(8,128)} all-to-all(f32[32,8,128]{2,1,0:T(8,128)S(1)} %broadcast_in_dim.14), channel_id=1, replica_groups=mesh['x'=4,'z'=8,'y'=8,'core'=2] {'x','y'}, dimensions={0} | all-to-all | bytes 262144 | tf_op jit(solution)/shard_map/all_to_all | solution.py:208
  171.0 7.1 %combine.1 = (f32[384,128]{1,0:T(8,128)}, f32[384,128]{1,0:T(8,128)}) custom-call(f32[32,8,128]{2,1,0:T(8,128)} %all_to_all.26.part_ref, f32[32,208,256]{2,1,0:T(8,128)} %get-tuple-element.13.refs_0_, f32[32,208,128]{2,1,0:T(8,128)} %get-tuple-element.14.refs_1_), custom_call_target="tpu_custom_call" | custom-call | tf_op jit(solution)/shard_map/combine/pallas_call | solution.py:210
  178.1 4.1 %collective-permute-start.15 = (f32[384,128]{1,0:T(8,128)}, f32[384,128]{1,0:T(8,128)S(1)}, u32[]{:S(2)}, u32[]{:S(2)}) collective-permute-start(f32[384,128]{1,0:T(8,128)} %get-tuple-element.16), channel_id=1, source_target_pairs={{0,1},{1,0},{2,3},{3,2},{4,5},{5,4},{6,7},{7,6},{8,9},{9,8},{10,11... | collective-permute-start | bytes 589832 | tf_op jit(solution)/shard_map/ppermute | solution.py:224
  184.5 14.8 %all_to_all.27.pieces_ref = f32[32,24,128]{2,1,0:T(8,128)S(1)} all-to-all(f32[32,24,128]{2,1,0:T(8,128)S(1)} %bitcast.13), channel_id=1, replica_groups=mesh['x'=4,'z'=8,'y'=8,'core'=2] {'x','z'}, dimensions={0} | all-to-all | bytes 786432 | tf_op jit(solution)/shard_map/all_to_all | solution.py:228
  (62 shorter events, 16.9 us)
Async XLA Ops:
  1.6 29.4 %all-to-all-start.1 = ((bf16[64,8,384]{2,1,0:T(8,128)(2,1)}), bf16[64,8,384]{2,1,0:T(8,128)(2,1)S(1)}, u32[]{:S(2)}, u32[]{:S(2)}) async-start(bf16[64,8,384]{2,1,0:T(8,128)(2,1)} %bitcast.4), calls=%async_computation.1 | async-start | bytes 786432 | tf_op jit(solution)/shard_map/all_to_all | solution.py:172
  31.0 26.1 %all-to-all-start = ((bf16[32,104,128]{2,1,0:T(8,128)(2,1)}), bf16[32,104,128]{2,1,0:T(8,128)(2,1)S(1)}, u32[]{:S(2)}, u32[]{:S(2)}) async-start(bf16[32,104,128]{2,1,0:T(8,128)(2,1)} %bitcast.1), calls=%async_computation | async-start | bytes 1703936 | tf_op jit(solution)/shard_map/all_to_all | solution.py:177
  36.2 75.0 %copy-start.2 = (bf16[512,256]{1,0:T(8,128)(2,1)}, bf16[512,256]{1,0:T(8,128)(2,1)S(1)}, u32[]{:S(2)}) copy-start(bf16[512,256]{1,0:T(8,128)(2,1)S(1)} %slice.8) | copy-start | bytes 786436
  36.2 32.6 %collective-permute-start.4 = (bf16[32,16,256]{2,1,0:T(8,128)(2,1)S(1)}, bf16[32,16,256]{2,1,0:T(8,128)(2,1)S(1)}, u32[]{:S(2)}, u32[]{:S(2)}) collective-permute-start(bf16[32,16,256]{2,1,0:T(8,128)(2,1)S(1)} %bitcast.14), channel_id=1, source_target_pairs={{0,2},{2,4},{4,6},{6,8},{8,10},{10,12},{12,14},{14,0},{1,3},{3,5},... | collective-permute-start | bytes 786440 | tf_op jit(solution)/shard_map/ppermute | solution.py:158
  57.1 53.9 %collective-permute-start = (bf16[32,104,128]{2,1,0:T(8,128)(2,1)S(1)}, bf16[32,104,128]{2,1,0:T(8,128)(2,1)S(1)}, u32[]{:S(2)}, u32[]{:S(2)}) collective-permute-start(bf16[32,104,128]{2,1,0:T(8,128)(2,1)S(1)} %all-to-all-done), channel_id=1, source_target_pairs={{0,1},{1,0},{2,3},{3,2},{4,5},{5,4},{6,7},{7,6},{8,9},{9,8},{10,11... | collective-permute-start | bytes 2555912 | tf_op jit(solution)/shard_map/ppermute | solution.py:178
  63.7 20.5 %collective-permute-start.1 = (bf16[32,16,256]{2,1,0:T(8,128)(2,1)S(1)}, bf16[32,16,256]{2,1,0:T(8,128)(2,1)S(1)}, u32[]{:S(2)}, u32[]{:S(2)}) collective-permute-start(bf16[32,16,256]{2,1,0:T(8,128)(2,1)S(1)} %bitcast.15), channel_id=1, source_target_pairs={{0,14},{2,0},{4,2},{6,4},{8,6},{10,8},{12,10},{14,12},{1,15},{3,1}... | collective-permute-start | bytes 786440 | tf_op jit(solution)/shard_map/ppermute | solution.py:160
  68.8 42.3 %copy-start.5 = (bf16[32,16,256]{2,1,0:T(8,128)(2,1)}, bf16[32,16,256]{2,1,0:T(8,128)(2,1)S(1)}, u32[]{:S(2)}) copy-start(bf16[32,16,256]{2,1,0:T(8,128)(2,1)S(1)} %collective-permute-done.4.refs_7_) | copy-start | bytes 786436
  68.8 20.0 %collective-permute-start.5 = (bf16[32,16,256]{2,1,0:T(8,128)(2,1)S(1)}, bf16[32,16,256]{2,1,0:T(8,128)(2,1)S(1)}, u32[]{:S(2)}, u32[]{:S(2)}) collective-permute-start(bf16[32,16,256]{2,1,0:T(8,128)(2,1)S(1)} %collective-permute-done.4.refs_7_), channel_id=1, source_target_pairs={{0,2},{2,4},{4,6},{6,8},{8,10},{10,12},{12,14},{14,0},{1,3},{3,5},... | collective-permute-start | bytes 786440 | tf_op jit(solution)/shard_map/ppermute | solution.py:158
  70.8 40.4 %copy-start.4 = (bf16[512,128]{1,0:T(8,128)(2,1)}, bf16[512,128]{1,0:T(8,128)(2,1)S(1)}, u32[]{:S(2)}) copy-start(bf16[512,128]{1,0:T(8,128)(2,1)S(1)} %slice.9) | copy-start | bytes 393220
  70.8 11.5 %collective-permute-start.11 = (bf16[32,16,128]{2,1,0:T(8,128)(2,1)S(1)}, bf16[32,16,128]{2,1,0:T(8,128)(2,1)S(1)}, u32[]{:S(2)}, u32[]{:S(2)}) collective-permute-start(bf16[32,16,128]{2,1,0:T(8,128)(2,1)S(1)} %bitcast.17), channel_id=1, source_target_pairs={{0,2},{2,4},{4,6},{6,8},{8,10},{10,12},{12,14},{14,0},{1,3},{3,5},... | collective-permute-start | bytes 393224 | tf_op jit(solution)/shard_map/ppermute | solution.py:158
  72.7 18.1 %collective-permute-start.8 = (bf16[32,16,128]{2,1,0:T(8,128)(2,1)S(1)}, bf16[32,16,128]{2,1,0:T(8,128)(2,1)S(1)}, u32[]{:S(2)}, u32[]{:S(2)}) collective-permute-start(bf16[32,16,128]{2,1,0:T(8,128)(2,1)S(1)} %bitcast.18), channel_id=1, source_target_pairs={{0,14},{2,0},{4,2},{6,4},{8,6},{10,8},{12,10},{14,12},{1,15},{3,1}... | collective-permute-start | bytes 393224 | tf_op jit(solution)/shard_map/ppermute | solution.py:160
  82.3 48.8 %copy-start.11 = (bf16[32,16,128]{2,1,0:T(8,128)(2,1)}, bf16[32,16,128]{2,1,0:T(8,128)(2,1)S(1)}, u32[]{:S(2)}) copy-start(bf16[32,16,128]{2,1,0:T(8,128)(2,1)S(1)} %collective-permute-done.11.refs_7_) | copy-start | bytes 393220
  82.3 13.1 %collective-permute-start.12 = (bf16[32,16,128]{2,1,0:T(8,128)(2,1)S(1)}, bf16[32,16,128]{2,1,0:T(8,128)(2,1)S(1)}, u32[]{:S(2)}, u32[]{:S(2)}) collective-permute-start(bf16[32,16,128]{2,1,0:T(8,128)(2,1)S(1)} %collective-permute-done.11.refs_7_), channel_id=1, source_target_pairs={{0,2},{2,4},{4,6},{6,8},{8,10},{10,12},{12,14},{14,0},{1,3},{3,5},... | collective-permute-start | bytes 393224 | tf_op jit(solution)/shard_map/ppermute | solution.py:158
  84.3 33.2 %copy-start.6 = (bf16[32,16,256]{2,1,0:T(8,128)(2,1)}, bf16[32,16,256]{2,1,0:T(8,128)(2,1)S(1)}, u32[]{:S(2)}) copy-start(bf16[32,16,256]{2,1,0:T(8,128)(2,1)S(1)} %collective-permute-done.1.refs_1_) | copy-start | bytes 786436
  84.3 20.1 %collective-permute-start.2 = (bf16[32,16,256]{2,1,0:T(8,128)(2,1)S(1)}, bf16[32,16,256]{2,1,0:T(8,128)(2,1)S(1)}, u32[]{:S(2)}, u32[]{:S(2)}) collective-permute-start(bf16[32,16,256]{2,1,0:T(8,128)(2,1)S(1)} %collective-permute-done.1.refs_1_), channel_id=1, source_target_pairs={{0,14},{2,0},{4,2},{6,4},{8,6},{10,8},{12,10},{14,12},{1,15},{3,1}... | collective-permute-start | bytes 786440 | tf_op jit(solution)/shard_map/ppermute | solution.py:160
  88.9 28.6 %copy-start.7 = (bf16[32,16,256]{2,1,0:T(8,128)(2,1)}, bf16[32,16,256]{2,1,0:T(8,128)(2,1)S(1)}, u32[]{:S(2)}) copy-start(bf16[32,16,256]{2,1,0:T(8,128)(2,1)S(1)} %collective-permute-done.5.refs_6_) | copy-start | bytes 786436
  88.9 20.1 %collective-permute-start.6 = (bf16[32,16,256]{2,1,0:T(8,128)(2,1)S(1)}, bf16[32,16,256]{2,1,0:T(8,128)(2,1)S(1)}, u32[]{:S(2)}, u32[]{:S(2)}) collective-permute-start(bf16[32,16,256]{2,1,0:T(8,128)(2,1)S(1)} %collective-permute-done.5.refs_6_), channel_id=1, source_target_pairs={{0,2},{2,4},{4,6},{6,8},{8,10},{10,12},{12,14},{14,0},{1,3},{3,5},... | collective-permute-start | bytes 786440 | tf_op jit(solution)/shard_map/ppermute | solution.py:158
  90.8 6.5 %collective-permute-start.9 = (bf16[32,16,128]{2,1,0:T(8,128)(2,1)S(1)}, bf16[32,16,128]{2,1,0:T(8,128)(2,1)}, u32[]{:S(2)}, u32[]{:S(2)}) collective-permute-start(bf16[32,16,128]{2,1,0:T(8,128)(2,1)S(1)} %collective-permute-done.8.refs_1_), channel_id=1, source_target_pairs={{0,14},{2,0},{4,2},{6,4},{8,6},{10,8},{12,10},{14,12},{1,15},{3,1}... | collective-permute-start | bytes 393224 | tf_op jit(solution)/shard_map/ppermute | solution.py:160
  95.4 7.0 %collective-permute-start.13 = (bf16[32,16,128]{2,1,0:T(8,128)(2,1)S(1)}, bf16[32,16,128]{2,1,0:T(8,128)(2,1)}, u32[]{:S(2)}, u32[]{:S(2)}) collective-permute-start(bf16[32,16,128]{2,1,0:T(8,128)(2,1)S(1)} %collective-permute-done.12.refs_6_), channel_id=1, source_target_pairs={{0,2},{2,4},{4,6},{6,8},{8,10},{10,12},{12,14},{14,0},{1,3},{3,5},... | collective-permute-start | bytes 393224 | tf_op jit(solution)/shard_map/ppermute | solution.py:158
  97.4 33.8 %collective-permute-start.10 = (bf16[32,16,128]{2,1,0:T(8,128)(2,1)}, bf16[32,16,128]{2,1,0:T(8,128)(2,1)}, u32[]{:S(2)}, u32[]{:S(2)}) collective-permute-start(bf16[32,16,128]{2,1,0:T(8,128)(2,1)} %collective-permute-done.9.refs_2_), channel_id=1, source_target_pairs={{0,14},{2,0},{4,2},{6,4},{8,6},{10,8},{12,10},{14,12},{1,15},{3,1}... | collective-permute-start | bytes 393224 | tf_op jit(solution)/shard_map/ppermute | solution.py:160
  102.5 28.7 %collective-permute-start.14 = (bf16[32,16,128]{2,1,0:T(8,128)(2,1)}, bf16[32,16,128]{2,1,0:T(8,128)(2,1)}, u32[]{:S(2)}, u32[]{:S(2)}) collective-permute-start(bf16[32,16,128]{2,1,0:T(8,128)(2,1)} %collective-permute-done.13.refs_5_), channel_id=1, source_target_pairs={{0,2},{2,4},{4,6},{6,8},{8,10},{10,12},{12,14},{14,0},{1,3},{3,5},... | collective-permute-start | bytes 393224 | tf_op jit(solution)/shard_map/ppermute | solution.py:158
  104.4 7.9 %collective-permute-start.3 = (bf16[32,16,256]{2,1,0:T(8,128)(2,1)S(1)}, bf16[32,16,256]{2,1,0:T(8,128)(2,1)S(1)}, u32[]{:S(2)}, u32[]{:S(2)}) collective-permute-start(bf16[32,16,256]{2,1,0:T(8,128)(2,1)S(1)} %collective-permute-done.2.refs_2_), channel_id=1, source_target_pairs={{0,14},{2,0},{4,2},{6,4},{8,6},{10,8},{12,10},{14,12},{1,15},{3,1}... | collective-permute-start | bytes 786440 | tf_op jit(solution)/shard_map/ppermute | solution.py:160
  109.0 8.4 %collective-permute-start.7 = (bf16[32,16,256]{2,1,0:T(8,128)(2,1)S(1)}, bf16[32,16,256]{2,1,0:T(8,128)(2,1)}, u32[]{:S(2)}, u32[]{:S(2)}) collective-permute-start(bf16[32,16,256]{2,1,0:T(8,128)(2,1)S(1)} %collective-permute-done.6.refs_5_), channel_id=1, source_target_pairs={{0,2},{2,4},{4,6},{6,8},{8,10},{10,12},{12,14},{14,0},{1,3},{3,5},... | collective-permute-start | bytes 786440 | tf_op jit(solution)/shard_map/ppermute | solution.py:158
  178.1 5.4 %collective-permute-start.15 = (f32[384,128]{1,0:T(8,128)}, f32[384,128]{1,0:T(8,128)S(1)}, u32[]{:S(2)}, u32[]{:S(2)}) collective-permute-start(f32[384,128]{1,0:T(8,128)} %get-tuple-element.16), channel_id=1, source_target_pairs={{0,1},{1,0},{2,3},{3,2},{4,5},{5,4},{6,7},{7,6},{8,9},{9,8},{10,11... | collective-permute-start | bytes 589832 | tf_op jit(solution)/shard_map/ppermute | solution.py:224
  (9 other events, 101.5 us)

commit v4 on v3

--- a/solution.py
+++ b/solution.py
@@ -1,11 +1,10 @@
-import functools
-
 import jax
 import jax.numpy as jnp
 from jax import lax
 from jax.experimental import pallas as pl
 from jax.experimental.pallas import tpu as pltpu
 from jax.sharding import Mesh, PartitionSpec as P
+
 
 EPSILON = 1e-06
 DECAY = 0.9
@@ -14,7 +13,7 @@
 LANES = 128
 XZ = ("x", "z")
 CORES = [(0, 1), (1, 0)]
-CHUNKS = ((0, 256), (256, 128))
+PIECES = ((0, 56), (56, 56), (112, 56), (168, 40))
 
 
 def gram_kernel(cols_ref, *refs):
@@ -108,37 +107,36 @@
     return w_col
 
 
-def combine_kernel(part_ref, *refs):
-    n = len(CHUNKS)
-    kept, (mine_ref, theirs_ref, w_ref, ct_ref) = refs[:n], refs[n : n + 4]
-    g_refs, sem = refs[n + 4 : -1], refs[-1]
-    share = g_refs[0].shape[1] // 2
-    loads = [pltpu.make_async_copy(kept[k], g_refs[k], sem.at[k]) for k in range(n)]
-    for load in loads:
-        load.start()
+def combine_kernel(part_ref, kept_ref, mine_ref, theirs_ref, w_ref, ct_ref, g_ref, sem):
+    share = kept_ref.shape[1] // 2
+    lane_blocks = kept_ref.shape[2] // LANES
+    loads = []
+    for k, (start, size) in enumerate(PIECES):
+        rows = pl.ds(start, size)
+        loads.append(pltpu.make_async_copy(kept_ref.at[:, rows], g_ref.at[:, rows], sem.at[k]))
+        loads[-1].start()
     weights = tree_weights(jnp.sum(part_ref[...], axis=0))
     for r in range(NR):
         w_ref[r] = jnp.broadcast_to(weights[r : r + 1, :], (8, LANES))
     ct_ref[pl.ds(2 * share, 48), :] = jnp.zeros((48, ct_ref.shape[1]), jnp.float32)
-    for load in loads:
-        load.wait()
-    blocks = [(g, lb) for g in g_refs for lb in range(g.shape[2] // LANES)]
 
     def body(f, carry):
         row = pl.multiple_of(f * 8, 8)
-        acc = [None] * len(blocks)
+        acc = [None] * lane_blocks
         for r in range(NR):
             weight = w_ref[r]
-            for k, (g, lb) in enumerate(blocks):
-                term = g[r, pl.ds(row, 8), lb * LANES : (lb + 1) * LANES] * weight
+            for k in range(lane_blocks):
+                term = g_ref[r, pl.ds(row, 8), k * LANES : (k + 1) * LANES] * weight
                 acc[k] = term if r == 0 else acc[k] + term
-        for k in range(len(blocks)):
+        for k in range(lane_blocks):
             ct_ref[pl.ds(row, 8), k * LANES : (k + 1) * LANES] = acc[k]
         return carry
 
-    lax.fori_loop(0, 2 * share // 8, body, 0)
+    for load, (start, size) in zip(loads, PIECES):
+        load.wait()
+        lax.fori_loop(start // 8, (start + size) // 8, body, 0)
     for part, ref in enumerate((mine_ref, theirs_ref)):
-        for k in range(len(blocks)):
+        for k in range(lane_blocks):
             lanes = slice(k * LANES, (k + 1) * LANES)
             ref[lanes, :] = ct_ref[share * part : share * part + LANES, lanes].T
 
@@ -174,34 +172,29 @@
 
     shift = 16 * lax.axis_index("y")
     rolled = lax.dynamic_slice_in_dim(jnp.concatenate([grad_out, grad_out], axis=0), shift, TOK, 0)
+    acts = ring(halves.reshape(NR, 16, depth))
     own = lax.all_to_all(rolled.T.reshape(NR, share, TOK), XZ, 0, 0, tiled=True)
     other = lax.ppermute(own, "core", CORES)
     cols = jnp.concatenate([own, other], axis=1)
 
-    grads, grams = [], []
-    for start, width in CHUNKS:
-        acts = ring(halves[:, start : start + width].reshape(NR, 16, width))
-        grad, gram = pl.pallas_call(
-            gram_kernel,
-            out_shape=[
-                jax.ShapeDtypeStruct((NR, 2 * share, width), jnp.float32),
-                jax.ShapeDtypeStruct((8, LANES), jnp.float32),
-            ],
-            out_specs=[
-                pl.BlockSpec(memory_space=pltpu.HBM),
-                pl.BlockSpec(memory_space=pltpu.VMEM),
-            ],
-            scratch_shapes=[
-                pltpu.VMEM((NR, 2 * share, width), jnp.float32),
-                pltpu.VMEM((1024, LANES), jnp.float32),
-                pltpu.SemaphoreType.DMA,
-            ],
-            compiler_params=pltpu.CompilerParams(vmem_limit_bytes=60 << 20),
-            name="gram",
-        )(cols, *acts)
-        grads.append(grad)
-        grams.append(gram)
-    gram = sum(grams)
+    grads, gram = pl.pallas_call(
+        gram_kernel,
+        out_shape=[
+            jax.ShapeDtypeStruct((NR, 2 * share, depth), jnp.float32),
+            jax.ShapeDtypeStruct((8, LANES), jnp.float32),
+        ],
+        out_specs=[
+            pl.BlockSpec(memory_space=pltpu.HBM),
+            pl.BlockSpec(memory_space=pltpu.VMEM),
+        ],
+        scratch_shapes=[
+            pltpu.VMEM((NR, 2 * share, depth), jnp.float32),
+            pltpu.VMEM((1024, LANES), jnp.float32),
+            pltpu.SemaphoreType.DMA,
+        ],
+        compiler_params=pltpu.CompilerParams(vmem_limit_bytes=60 << 20),
+        name="gram",
+    )(cols, *acts)
 
     gram = lax.all_to_all(jnp.broadcast_to(gram, (16, 8, LANES)), ("z", "core"), 0, 0, tiled=True)
     gram = jnp.sum(gram, axis=0)
@@ -213,14 +206,16 @@
         scratch_shapes=[
             pltpu.VMEM((NR, 8, LANES), jnp.float32),
             pltpu.VMEM((256, depth), jnp.float32),
-            *(pltpu.VMEM(g.shape, jnp.float32) for g in grads),
-            pltpu.SemaphoreType.DMA((len(grads),)),
-        ],
-        in_specs=[pl.BlockSpec(memory_space=pltpu.VMEM)]
-        + [pl.BlockSpec(memory_space=pltpu.HBM)] * len(grads),
+            pltpu.VMEM(grads.shape, jnp.float32),
+            pltpu.SemaphoreType.DMA((len(PIECES),)),
+        ],
+        in_specs=[
+            pl.BlockSpec(memory_space=pltpu.VMEM),
+            pl.BlockSpec(memory_space=pltpu.HBM),
+        ],
         compiler_params=pltpu.CompilerParams(vmem_limit_bytes=60 << 20),
         name="combine",
-    )(gram, *grads)
+    )(gram, grads)
     came = lax.ppermute(theirs, "core", CORES)
     low = jnp.where(core == 0, mine, came)
     high = jnp.where(core == 0, came, mine)
@@ -239,6 +234,7 @@
     devices = mesh.devices.reshape(4, 8, 8, 2)
     fine = Mesh(devices, ("x", "z", "y", "core"))
     dp, hidden = ("x", "z"), ("y", "core")
+
     return jax.shard_map(
         local,
         mesh=fine,

time: 203 us -> 173 us (0.85)
  starting transfers between devices: 75.8 us -> 53.9 us
  Pallas kernels: 30.3 us -> 25.7 us
  blocking collectives: 45.1 us -> 42 us
    ppermute x6 -> x3, starting transfers between devices: 28.4 us -> 14.2 us  [ring(): above.append(lax.ppermute(above[-1], 'y', down))]
    all_to_all x1, waiting for transfers between devices: 17.7 us -> 5.32 us  [local(): own = lax.all_to_all(rolled.T.reshape(NR, share, TOK), XZ, 0, 0, tiled=True)]
    ppermute x6 -> x3, waiting for transfers between devices: 1.08 us -> 10.8 us  [ring(): above.append(lax.ppermute(above[-1], 'y', down))]
    ppermute x8 -> x4, starting transfers between devices: 16.6 us -> 8.96 us  [ring(): below.append(lax.ppermute(below[-1], 'y', up))]
    pallas_call x2 -> x1, Pallas kernels: 22.4 us -> 18.7 us  [local(): pl.pallas_call(gram_kernel, out_shape=[jax.ShapeDtypeStruct((NR, 2 * shar...]
    all_to_all x1, blocking collectives: 16.2 us -> 13.1 us  [local(): lax.all_to_all(jnp.broadcast_to(gram, (16, 8, LANES)), ('z', 'core'), 0,...]
    ppermute x8 -> x4, waiting for transfers between devices: 9.51 us -> 11.8 us  [ring(): below.append(lax.ppermute(below[-1], 'y', up))]
  transfers between devices with their start and end apart: 18 -> 11, of which waited for: 6 -> 7; matrix products, arithmetic and copies ran while one was open for 1% -> 2% of each run, Pallas kernels for 7% -> 0%
where the time goes in v4:
time: 173 us; the launch traced here: 170 us
  starting transfers between devices  53.9 us (31%)
  waiting for transfers between devices  42.1 us (24%)
  blocking collectives  42 us (24%)
  Pallas kernels  25.7 us (15%)
  local copies, waits for them, and re-layouts  3.57 us (2%)
  other arithmetic  2.74 us (2%)
    pallas_call x1, Pallas kernels, local(): pl.pallas_call(gram_kernel, out_shape=[jax.ShapeDtypeStruct((NR, 2 * shar...  18.7 us
    all_to_all x1, starting transfers between devices, local(): halves = lax.all_to_all(halves, ('x', 'z', 'core'), 0, 0, tiled=True)  14.8 us
    all_to_all x1, blocking collectives, local(): pieces = lax.all_to_all(pieces, XZ, 0, 0, tiled=True)  14.8 us
    ppermute x3, starting transfers between devices, ring(): above.append(lax.ppermute(above[-1], 'y', down))  14.2 us
    all_to_all x1, blocking collectives, local(): lax.all_to_all(jnp.broadcast_to(gram, (32, 8, LANES)), ('x', 'y'), 0, 0,...  14.2 us
    all_to_all x1, blocking collectives, local(): lax.all_to_all(jnp.broadcast_to(gram, (16, 8, LANES)), ('z', 'core'), 0,...  13.1 us
    all_to_all x1, waiting for transfers between devices, local(): halves = lax.all_to_all(halves, ('x', 'z', 'core'), 0, 0, tiled=True)  12.9 us
    ppermute x4, waiting for transfers between devices, ring(): below.append(lax.ppermute(below[-1], 'y', up))  11.8 us
  transfers between devices with their start and end apart: 11, of which 7 were waited for; matrix products, arithmetic and copies ran while one was open for 2% of the time, Pallas kernels for 0%

profile of v4, /device:TPU:1, one launch (start us, length us, event | category | flops | bytes accessed | tf_op | source)
XLA Modules:
  0.0 170.2 jit_solution(17990008748541307156)
XLA Ops:
  0.0 1.6 broadcast_in_dim.12
  1.6 14.8 %all-to-all-start.1 = ((bf16[64,8,384]{2,1,0:T(8,128)(2,1)}), bf16[64,8,384]{2,1,0:T(8,128)(2,1)S(1)}, u32[]{:S(2)}, u32[]{:S(2)}) async-start(bf16[64,8,384]{2,1,0:T(8,128)(2,1)} %bitcast.4), calls=%async_computation.1 | async-start | bytes 786432 | tf_op jit(solution)/shard_map/all_to_all | solution.py:170
  18.1 12.9 %all-to-all-done.1 = bf16[64,8,384]{2,1,0:T(8,128)(2,1)S(1)} async-done(((bf16[64,8,384]{2,1,0:T(8,128)(2,1)}), bf16[64,8,384]{2,1,0:T(8,128)(2,1)S(1)}, u32[]{:S(2)}, u32[]{:S(2)}) %all-to-all-start.1) | async-done | bytes 393248 | tf_op jit(solution)/shard_map/all_to_all | solution.py:170
  31.0 5.2 %all-to-all-start = ((bf16[32,104,128]{2,1,0:T(8,128)(2,1)}), bf16[32,104,128]{2,1,0:T(8,128)(2,1)S(1)}, u32[]{:S(2)}, u32[]{:S(2)}) async-start(bf16[32,104,128]{2,1,0:T(8,128)(2,1)} %bitcast.1), calls=%async_computation | async-start | bytes 1703936 | tf_op jit(solution)/shard_map/all_to_all | solution.py:176
  36.2 3.2 %collective-permute-start.4 = (bf16[32,16,384]{2,1,0:T(8,128)(2,1)S(1)}, bf16[32,16,384]{2,1,0:T(8,128)(2,1)S(1)}, u32[]{:S(2)}, u32[]{:S(2)}) collective-permute-start(bf16[32,16,384]{2,1,0:T(8,128)(2,1)S(1)} %bitcast.9), channel_id=1, source_target_pairs={{0,2},{2,4},{4,6},{6,8},{8,10},{10,12},{12,14},{14,0},{1,3},{3,5},... | collective-permute-start | bytes 1179656 | tf_op jit(solution)/shard_map/ppermute | solution.py:156
  39.4 3.8 %collective-permute-start.1 = (bf16[32,16,384]{2,1,0:T(8,128)(2,1)S(1)}, bf16[32,16,384]{2,1,0:T(8,128)(2,1)S(1)}, u32[]{:S(2)}, u32[]{:S(2)}) collective-permute-start(bf16[32,16,384]{2,1,0:T(8,128)(2,1)S(1)} %bitcast.10), channel_id=1, source_target_pairs={{0,14},{2,0},{4,2},{6,4},{8,6},{10,8},{12,10},{14,12},{1,15},{3,1}... | collective-permute-start | bytes 1179656 | tf_op jit(solution)/shard_map/ppermute | solution.py:158
  43.2 6.7 %collective-permute-done.4.refs_7_ = bf16[32,16,384]{2,1,0:T(8,128)(2,1)S(1)} collective-permute-done((bf16[32,16,384]{2,1,0:T(8,128)(2,1)S(1)}, bf16[32,16,384]{2,1,0:T(8,128)(2,1)S(1)}, u32[]{:S(2)}, u32[]{:S(2)}) %collective-permute-start.4) | collective-permute-done | bytes 393248 | tf_op jit(solution)/shard_map/ppermute | solution.py:156
  49.9 1.9 %collective-permute-start.5 = (bf16[32,16,384]{2,1,0:T(8,128)(2,1)S(1)}, bf16[32,16,384]{2,1,0:T(8,128)(2,1)S(1)}, u32[]{:S(2)}, u32[]{:S(2)}) collective-permute-start(bf16[32,16,384]{2,1,0:T(8,128)(2,1)S(1)} %collective-permute-done.4.refs_7_), channel_id=1, source_target_pairs={{0,2},{2,4},{4,6},{6,8},{8,10},{10,12},{12,14},{14,0},{1,3},{3,5},... | collective-permute-start | bytes 1179656 | tf_op jit(solution)/shard_map/ppermute | solution.py:156
  51.8 5.3 %all-to-all-done = bf16[32,104,128]{2,1,0:T(8,128)(2,1)S(1)} async-done(((bf16[32,104,128]{2,1,0:T(8,128)(2,1)}), bf16[32,104,128]{2,1,0:T(8,128)(2,1)S(1)}, u32[]{:S(2)}, u32[]{:S(2)}) %all-to-all-start) | async-done | bytes 852000 | tf_op jit(solution)/shard_map/all_to_all | solution.py:176
  57.1 6.6 %collective-permute-start = (bf16[32,104,128]{2,1,0:T(8,128)(2,1)S(1)}, bf16[32,104,128]{2,1,0:T(8,128)(2,1)S(1)}, u32[]{:S(2)}, u32[]{:S(2)}) collective-permute-start(bf16[32,104,128]{2,1,0:T(8,128)(2,1)S(1)} %all-to-all-done), channel_id=1, source_target_pairs={{0,1},{1,0},{2,3},{3,2},{4,5},{5,4},{6,7},{7,6},{8,9},{9,8},{10,11... | collective-permute-start | bytes 2555912 | tf_op jit(solution)/shard_map/ppermute | solution.py:177
  63.7 5.1 %collective-permute-start.2 = (bf16[32,16,384]{2,1,0:T(8,128)(2,1)S(1)}, bf16[32,16,384]{2,1,0:T(8,128)(2,1)S(1)}, u32[]{:S(2)}, u32[]{:S(2)}) collective-permute-start(bf16[32,16,384]{2,1,0:T(8,128)(2,1)S(1)} %collective-permute-done.1.refs_1_), channel_id=1, source_target_pairs={{0,14},{2,0},{4,2},{6,4},{8,6},{10,8},{12,10},{14,12},{1,15},{3,1}... | collective-permute-start | bytes 1179656 | tf_op jit(solution)/shard_map/ppermute | solution.py:158
  68.9 1.9 %collective-permute-start.6 = (bf16[32,16,384]{2,1,0:T(8,128)(2,1)S(1)}, bf16[32,16,384]{2,1,0:T(8,128)(2,1)S(1)}, u32[]{:S(2)}, u32[]{:S(2)}) collective-permute-start(bf16[32,16,384]{2,1,0:T(8,128)(2,1)S(1)} %collective-permute-done.5.refs_6_), channel_id=1, source_target_pairs={{0,2},{2,4},{4,6},{6,8},{8,10},{10,12},{12,14},{14,0},{1,3},{3,5},... | collective-permute-start | bytes 1179656 | tf_op jit(solution)/shard_map/ppermute | solution.py:156
  70.8 6.5 %collective-permute-done.2.refs_2_ = bf16[32,16,384]{2,1,0:T(8,128)(2,1)S(1)} collective-permute-done((bf16[32,16,384]{2,1,0:T(8,128)(2,1)S(1)}, bf16[32,16,384]{2,1,0:T(8,128)(2,1)S(1)}, u32[]{:S(2)}, u32[]{:S(2)}) %collective-permute-start.2) | collective-permute-done | bytes 393248 | tf_op jit(solution)/shard_map/ppermute | solution.py:158
  77.3 5.3 %collective-permute-start.3 = (bf16[32,16,384]{2,1,0:T(8,128)(2,1)S(1)}, bf16[32,16,384]{2,1,0:T(8,128)(2,1)S(1)}, u32[]{:S(2)}, u32[]{:S(2)}) collective-permute-start(bf16[32,16,384]{2,1,0:T(8,128)(2,1)S(1)} %collective-permute-done.2.refs_2_), channel_id=1, source_target_pairs={{0,14},{2,0},{4,2},{6,4},{8,6},{10,8},{12,10},{14,12},{1,15},{3,1}... | collective-permute-start | bytes 1179656 | tf_op jit(solution)/shard_map/ppermute | solution.py:158
  82.6 1.9 %collective-permute-start.7 = (bf16[32,16,384]{2,1,0:T(8,128)(2,1)S(1)}, bf16[32,16,384]{2,1,0:T(8,128)(2,1)}, u32[]{:S(2)}, u32[]{:S(2)}) collective-permute-start(bf16[32,16,384]{2,1,0:T(8,128)(2,1)S(1)} %collective-permute-done.6.refs_5_), channel_id=1, source_target_pairs={{0,2},{2,4},{4,6},{6,8},{8,10},{10,12},{12,14},{14,0},{1,3},{3,5},... | collective-permute-start | bytes 1179656 | tf_op jit(solution)/shard_map/ppermute | solution.py:156
  84.6 1.3 pad_maximum_fusion.cols_ref
  85.9 4.3 %collective-permute-done.3.refs_3_ = bf16[32,16,384]{2,1,0:T(8,128)(2,1)S(1)} collective-permute-done((bf16[32,16,384]{2,1,0:T(8,128)(2,1)S(1)}, bf16[32,16,384]{2,1,0:T(8,128)(2,1)S(1)}, u32[]{:S(2)}, u32[]{:S(2)}) %collective-permute-start.3) | collective-permute-done | bytes 393248 | tf_op jit(solution)/shard_map/ppermute | solution.py:158
  90.2 5.2 %collective-permute-done.7.refs_4_ = bf16[32,16,384]{2,1,0:T(8,128)(2,1)} collective-permute-done((bf16[32,16,384]{2,1,0:T(8,128)(2,1)S(1)}, bf16[32,16,384]{2,1,0:T(8,128)(2,1)}, u32[]{:S(2)}, u32[]{:S(2)}) %collective-permute-start.7) | collective-permute-done | bytes 393248 | tf_op jit(solution)/shard_map/ppermute | solution.py:156
  95.4 18.7 %gram.1 = (f32[32,208,384]{2,1,0:T(8,128)}, f32[8,128]{1,0:T(8,128)}) custom-call(bf16[32,208,128]{2,1,0:T(8,128)(2,1)} %pad_maximum_fusion.cols_ref, bf16[32,16,384]{2,1,0:T(8,128)(2,1)} %bitcast.11, bf16[32,16,384]{2,1,0:T(8,128)(2,1)} %copy-done.4, bf16[32,16,384]{2,1,0:T(8,128)(2,1)} %copy-done.6, bf16[32,16,384]{2,1,0:T(8,128)(2,1)} %copy-done.8, ...), custom_call_target="tpu_custom_call" | custom-call | tf_op jit(solution)/shard_map/gram/pallas_call | solution.py:180
  114.8 13.1 %all_to_all.25 = f32[16,8,128]{2,1,0:T(8,128)S(1)} all-to-all(f32[16,8,128]{2,1,0:T(8,128)S(1)} %broadcast_in_dim.13), channel_id=1, replica_groups=mesh['x'=4,'z'=8,'y'=8,'core'=2] {'z','core'}, dimensions={0} | all-to-all | bytes 131072 | tf_op jit(solution)/shard_map/all_to_all | solution.py:199
  127.9 14.2 %all_to_all.26.part_ref = f32[32,8,128]{2,1,0:T(8,128)} all-to-all(f32[32,8,128]{2,1,0:T(8,128)S(1)} %broadcast_in_dim.14), channel_id=1, replica_groups=mesh['x'=4,'z'=8,'y'=8,'core'=2] {'x','y'}, dimensions={0} | all-to-all | bytes 262144 | tf_op jit(solution)/shard_map/all_to_all | solution.py:201
  142.1 6.1 %combine.1 = (f32[384,128]{1,0:T(8,128)}, f32[384,128]{1,0:T(8,128)}) custom-call(f32[32,8,128]{2,1,0:T(8,128)} %all_to_all.26.part_ref, f32[32,208,384]{2,1,0:T(8,128)} %get-tuple-element.10.kept_ref), custom_call_target="tpu_custom_call" | custom-call | tf_op jit(solution)/shard_map/combine/pallas_call | solution.py:203
  148.2 4.1 %collective-permute-start.8 = (f32[384,128]{1,0:T(8,128)}, f32[384,128]{1,0:T(8,128)S(1)}, u32[]{:S(2)}, u32[]{:S(2)}) collective-permute-start(f32[384,128]{1,0:T(8,128)} %get-tuple-element.12), channel_id=1, source_target_pairs={{0,1},{1,0},{2,3},{3,2},{4,5},{5,4},{6,7},{7,6},{8,9},{9,8},{10,11... | collective-permute-start | bytes 589832 | tf_op jit(solution)/shard_map/ppermute | solution.py:219
  154.6 14.8 %all_to_all.27.pieces_ref = f32[32,24,128]{2,1,0:T(8,128)S(1)} all-to-all(f32[32,24,128]{2,1,0:T(8,128)S(1)} %bitcast.12), channel_id=1, replica_groups=mesh['x'=4,'z'=8,'y'=8,'core'=2] {'x','z'}, dimensions={0} | all-to-all | bytes 786432 | tf_op jit(solution)/shard_map/all_to_all | solution.py:223
  (31 shorter events, 5.6 us)
Async XLA Ops:
  0.0 16.4 %copy-start.2 = (bf16[128,3328]{1,0:T(8,128)(2,1)S(1)}, bf16[128,3328]{1,0:T(8,128)(2,1)}, u32[]{:S(2)}) copy-start(bf16[128,3328]{1,0:T(8,128)(2,1)} %param.4) | copy-start | bytes 2555908
  1.6 29.4 %all-to-all-start.1 = ((bf16[64,8,384]{2,1,0:T(8,128)(2,1)}), bf16[64,8,384]{2,1,0:T(8,128)(2,1)S(1)}, u32[]{:S(2)}, u32[]{:S(2)}) async-start(bf16[64,8,384]{2,1,0:T(8,128)(2,1)} %bitcast.4), calls=%async_computation.1 | async-start | bytes 786432 | tf_op jit(solution)/shard_map/all_to_all | solution.py:170
  31.0 54.9 %copy-start.1 = (bf16[64,8,384]{2,1,0:T(8,128)(2,1)}, bf16[64,8,384]{2,1,0:T(8,128)(2,1)S(1)}, u32[]{:S(2)}) copy-start(bf16[64,8,384]{2,1,0:T(8,128)(2,1)S(1)} %all-to-all-done.1) | copy-start | bytes 1179652
  31.0 26.1 %all-to-all-start = ((bf16[32,104,128]{2,1,0:T(8,128)(2,1)}), bf16[32,104,128]{2,1,0:T(8,128)(2,1)S(1)}, u32[]{:S(2)}, u32[]{:S(2)}) async-start(bf16[32,104,128]{2,1,0:T(8,128)(2,1)} %bitcast.1), calls=%async_computation | async-start | bytes 1703936 | tf_op jit(solution)/shard_map/all_to_all | solution.py:176
  36.2 13.7 %collective-permute-start.4 = (bf16[32,16,384]{2,1,0:T(8,128)(2,1)S(1)}, bf16[32,16,384]{2,1,0:T(8,128)(2,1)S(1)}, u32[]{:S(2)}, u32[]{:S(2)}) collective-permute-start(bf16[32,16,384]{2,1,0:T(8,128)(2,1)S(1)} %bitcast.9), channel_id=1, source_target_pairs={{0,2},{2,4},{4,6},{6,8},{8,10},{10,12},{12,14},{14,0},{1,3},{3,5},... | collective-permute-start | bytes 1179656 | tf_op jit(solution)/shard_map/ppermute | solution.py:156
  39.4 24.3 %collective-permute-start.1 = (bf16[32,16,384]{2,1,0:T(8,128)(2,1)S(1)}, bf16[32,16,384]{2,1,0:T(8,128)(2,1)S(1)}, u32[]{:S(2)}, u32[]{:S(2)}) collective-permute-start(bf16[32,16,384]{2,1,0:T(8,128)(2,1)S(1)} %bitcast.10), channel_id=1, source_target_pairs={{0,14},{2,0},{4,2},{6,4},{8,6},{10,8},{12,10},{14,12},{1,15},{3,1}... | collective-permute-start | bytes 1179656 | tf_op jit(solution)/shard_map/ppermute | solution.py:158
  49.9 45.5 %copy-start.3 = (bf16[32,16,384]{2,1,0:T(8,128)(2,1)}, bf16[32,16,384]{2,1,0:T(8,128)(2,1)S(1)}, u32[]{:S(2)}) copy-start(bf16[32,16,384]{2,1,0:T(8,128)(2,1)S(1)} %collective-permute-done.4.refs_7_) | copy-start | bytes 1179652
  49.9 19.0 %collective-permute-start.5 = (bf16[32,16,384]{2,1,0:T(8,128)(2,1)S(1)}, bf16[32,16,384]{2,1,0:T(8,128)(2,1)S(1)}, u32[]{:S(2)}, u32[]{:S(2)}) collective-permute-start(bf16[32,16,384]{2,1,0:T(8,128)(2,1)S(1)} %collective-permute-done.4.refs_7_), channel_id=1, source_target_pairs={{0,2},{2,4},{4,6},{6,8},{8,10},{10,12},{12,14},{14,0},{1,3},{3,5},... | collective-permute-start | bytes 1179656 | tf_op jit(solution)/shard_map/ppermute | solution.py:156
  57.1 27.4 %collective-permute-start = (bf16[32,104,128]{2,1,0:T(8,128)(2,1)S(1)}, bf16[32,104,128]{2,1,0:T(8,128)(2,1)S(1)}, u32[]{:S(2)}, u32[]{:S(2)}) collective-permute-start(bf16[32,104,128]{2,1,0:T(8,128)(2,1)S(1)} %all-to-all-done), channel_id=1, source_target_pairs={{0,1},{1,0},{2,3},{3,2},{4,5},{5,4},{6,7},{7,6},{8,9},{9,8},{10,11... | collective-permute-start | bytes 2555912 | tf_op jit(solution)/shard_map/ppermute | solution.py:177
  63.7 31.6 %copy-start.4 = (bf16[32,16,384]{2,1,0:T(8,128)(2,1)}, bf16[32,16,384]{2,1,0:T(8,128)(2,1)S(1)}, u32[]{:S(2)}) copy-start(bf16[32,16,384]{2,1,0:T(8,128)(2,1)S(1)} %collective-permute-done.1.refs_1_) | copy-start | bytes 1179652
  63.7 13.5 %collective-permute-start.2 = (bf16[32,16,384]{2,1,0:T(8,128)(2,1)S(1)}, bf16[32,16,384]{2,1,0:T(8,128)(2,1)S(1)}, u32[]{:S(2)}, u32[]{:S(2)}) collective-permute-start(bf16[32,16,384]{2,1,0:T(8,128)(2,1)S(1)} %collective-permute-done.1.refs_1_), channel_id=1, source_target_pairs={{0,14},{2,0},{4,2},{6,4},{8,6},{10,8},{12,10},{14,12},{1,15},{3,1}... | collective-permute-start | bytes 1179656 | tf_op jit(solution)/shard_map/ppermute | solution.py:158
  68.9 26.5 %copy-start.5 = (bf16[32,16,384]{2,1,0:T(8,128)(2,1)}, bf16[32,16,384]{2,1,0:T(8,128)(2,1)S(1)}, u32[]{:S(2)}) copy-start(bf16[32,16,384]{2,1,0:T(8,128)(2,1)S(1)} %collective-permute-done.5.refs_6_) | copy-start | bytes 1179652
  68.9 13.7 %collective-permute-start.6 = (bf16[32,16,384]{2,1,0:T(8,128)(2,1)S(1)}, bf16[32,16,384]{2,1,0:T(8,128)(2,1)S(1)}, u32[]{:S(2)}, u32[]{:S(2)}) collective-permute-start(bf16[32,16,384]{2,1,0:T(8,128)(2,1)S(1)} %collective-permute-done.5.refs_6_), channel_id=1, source_target_pairs={{0,2},{2,4},{4,6},{6,8},{8,10},{10,12},{12,14},{14,0},{1,3},{3,5},... | collective-permute-start | bytes 1179656 | tf_op jit(solution)/shard_map/ppermute | solution.py:156
  77.3 18.1 %copy-start.6 = (bf16[32,16,384]{2,1,0:T(8,128)(2,1)}, bf16[32,16,384]{2,1,0:T(8,128)(2,1)S(1)}, u32[]{:S(2)}) copy-start(bf16[32,16,384]{2,1,0:T(8,128)(2,1)S(1)} %collective-permute-done.2.refs_2_) | copy-start | bytes 1179652
  77.3 12.9 %collective-permute-start.3 = (bf16[32,16,384]{2,1,0:T(8,128)(2,1)S(1)}, bf16[32,16,384]{2,1,0:T(8,128)(2,1)S(1)}, u32[]{:S(2)}, u32[]{:S(2)}) collective-permute-start(bf16[32,16,384]{2,1,0:T(8,128)(2,1)S(1)} %collective-permute-done.2.refs_2_), channel_id=1, source_target_pairs={{0,14},{2,0},{4,2},{6,4},{8,6},{10,8},{12,10},{14,12},{1,15},{3,1}... | collective-permute-start | bytes 1179656 | tf_op jit(solution)/shard_map/ppermute | solution.py:158
  82.6 12.8 %copy-start.7 = (bf16[32,16,384]{2,1,0:T(8,128)(2,1)}, bf16[32,16,384]{2,1,0:T(8,128)(2,1)S(1)}, u32[]{:S(2)}) copy-start(bf16[32,16,384]{2,1,0:T(8,128)(2,1)S(1)} %collective-permute-done.6.refs_5_) | copy-start | bytes 1179652
  82.6 12.7 %collective-permute-start.7 = (bf16[32,16,384]{2,1,0:T(8,128)(2,1)S(1)}, bf16[32,16,384]{2,1,0:T(8,128)(2,1)}, u32[]{:S(2)}, u32[]{:S(2)}) collective-permute-start(bf16[32,16,384]{2,1,0:T(8,128)(2,1)S(1)} %collective-permute-done.6.refs_5_), channel_id=1, source_target_pairs={{0,2},{2,4},{4,6},{6,8},{8,10},{10,12},{12,14},{14,0},{1,3},{3,5},... | collective-permute-start | bytes 1179656 | tf_op jit(solution)/shard_map/ppermute | solution.py:156
  90.2 5.2 %copy-start.8 = (bf16[32,16,384]{2,1,0:T(8,128)(2,1)}, bf16[32,16,384]{2,1,0:T(8,128)(2,1)S(1)}, u32[]{:S(2)}) copy-start(bf16[32,16,384]{2,1,0:T(8,128)(2,1)S(1)} %collective-permute-done.3.refs_3_) | copy-start | bytes 1179652
  148.2 21.2 %copy-start = (f32[24,3328]{1,0:T(8,128)S(1)}, f32[24,3328]{1,0:T(8,128)}, u32[]{:S(2)}) copy-start(f32[24,3328]{1,0:T(8,128)} %momentum_ref.1) | copy-start | bytes 958468
  148.2 5.4 %collective-permute-start.8 = (f32[384,128]{1,0:T(8,128)}, f32[384,128]{1,0:T(8,128)S(1)}, u32[]{:S(2)}, u32[]{:S(2)}) collective-permute-start(f32[384,128]{1,0:T(8,128)} %get-tuple-element.12), channel_id=1, source_target_pairs={{0,1},{1,0},{2,3},{3,2},{4,5},{5,4},{6,7},{7,6},{8,9},{9,8},{10,11... | collective-permute-start | bytes 589832 | tf_op jit(solution)/shard_map/ppermute | solution.py:219
